TPU v7x, 32 devices: a whole 2x2x4 slice. The times are simulated.
32 devices in a mesh: row: 4 (over z), col: 8 (over y, x, core).
Axes of the slice: x: 2, y: 2, z: 4, core: 2. Of those that a mesh axis runs over, the one named last changes fastest.
Arguments:
- leaf_density: float32 [296, 262144], P(None, ('row', 'col')), may hold values from -6 to 6
- m2m: float32 [8, 296, 296], replicated, may hold values from -0.125 to 0.125
- v_source: int32 [512, 22], P(('row', 'col')), may hold values from 0 to 511, as said below
- v_class: int32 [512, 22], P(('row', 'col')), may hold values from 0 to 315
Outputs:
- coarse_density: float32 [296, 512], P(None, ('row', 'col'))
- far_field: float32 [296, 32768], P(None, ('row', 'col'))
Inputs may be any that keep to these rules, and one draw needn't show every extreme that they name: Box b is held by the device that holds row b of v_source. For two different devices, the V-lists of one device's boxes name at most 2 distinct boxes of the other; those of each device name exactly 2 boxes of the next device in order.
All inputs are finite; a program needn't handle non-finite values.
Results may differ from a plain program's by a relative error of at most 0.0003.
Values sent between devices are 32-bit elements; how exact they have to be, the bound alone decides.
No kernel may reach another device: no remote copies, remote signals or barrier semaphores. Data moves between devices by JAX's collectives and lax.ppermute only.
A program may use at most 192 MiB of HBM per device.

v0:
```python
import math

import jax
import jax.numpy as jnp
import numpy as np
from jax import lax
from jax.sharding import PartitionSpec as P

S = 296
R = 64
VL = 22
CAP = 2
CLASSES = 316
PAR_DEV = 16


radius = 0.525
kernel_scale = 1.0 / (4.0 * math.pi)


def from_partner(value, axis, distance):
    mask = 2**distance
    pairs = [(source, source ^ mask) for source in range(lax.axis_size(axis))]
    return lax.ppermute(value, axis, pairs)


def surface_points():
    edge_count = 2
    while edge_count**3 - (edge_count - 2) ** 3 != S:
        edge_count += 1
    coords = np.linspace(-1.0, 1.0, edge_count)
    lattice = np.stack(np.meshgrid(coords, coords, coords, indexing="ij"), -1).reshape(-1, 3)
    border = np.max(np.abs(lattice), axis=1) > 1.0 - 1e-09
    return lattice[border]


def offset_table():
    coords = np.arange(-3, 4)
    lattice = np.stack(np.meshgrid(coords, coords, coords, indexing="ij"), -1).reshape(-1, 3)
    farther = np.max(np.abs(lattice), axis=1) >= 2
    return lattice[farther]


def build_tiles(classes):
    highest = lax.Precision.HIGHEST
    table_arr = jnp.asarray(offset_table(), jnp.float32)
    one_hot = (classes[:, None] == jnp.arange(CLASSES, dtype=jnp.int32)[None, :]).astype(
        jnp.float32
    )
    offset = jnp.dot(one_hot, table_arr, precision=highest)
    points = jnp.asarray(surface_points() * radius, jnp.float32)
    dist_sq = jnp.zeros((classes.shape[0], S, S), jnp.float32)
    for comp in range(3):
        coord_pts = points[:, comp]
        delta = coord_pts[None, :, None] - offset[:, comp][:, None, None] - coord_pts[None, None, :]
        dist_sq = dist_sq + delta * delta
    return lax.rsqrt(dist_sq) * kernel_scale


def body(leaf_density, m2m, v_source, v_class):
    highest = lax.Precision.HIGHEST
    box_count = v_source.shape[0]
    leaves = leaf_density.reshape(S, box_count, 8, R)
    box_dens = jnp.einsum("cij,jbcr->ibr", m2m, leaves, precision=highest)
    device = lax.axis_index(("row", "col"))
    ndev = lax.axis_size(("row", "col"))
    global_ids = device * box_count + jnp.arange(box_count, dtype=jnp.int32)
    first_pos = global_ids % 8
    second_pos = global_ids // 8 % 8
    section_one = jnp.einsum(
        "bij,jbr->ibr", jnp.take(m2m, first_pos, axis=0), box_dens, precision=highest
    )
    partial_value = jnp.einsum(
        "bij,jbr->ir", jnp.take(m2m, second_pos, axis=0), section_one, precision=highest
    )
    group_size = 64 // PAR_DEV
    bit_count = group_size.bit_length() - 1
    share_cols = R // group_size
    member = device % group_size
    current = partial_value
    for section in range(bit_count):
        current = current + from_partner(current, ("row", "col"), section)
    coarse_part = lax.dynamic_slice_in_dim(current, member * share_cols, share_cols, 1)
    owners = v_source // box_count
    local_idx = v_source % box_count
    ref_match = (
        v_source.reshape(-1)[:, None] == jnp.arange(ndev * box_count, dtype=jnp.int32)[None, :]
    )
    needed = jnp.any(ref_match, axis=0).reshape(ndev, box_count)
    needed = needed & (jnp.arange(ndev, dtype=jnp.int32)[:, None] != device)
    slot_rank = jnp.cumsum(needed.astype(jnp.int32), axis=1) - 1
    slot_hit = needed[:, None, :] & (
        slot_rank[:, None, :] == jnp.arange(CAP, dtype=jnp.int32)[None, :, None]
    )
    local_range = jnp.arange(box_count, dtype=jnp.int32)[None, None, :]
    wanted = jnp.where(jnp.any(slot_hit, axis=2), jnp.sum(slot_hit * local_range, axis=2), -1)
    requested = lax.all_to_all(wanted, ("row", "col"), split_axis=0, concat_axis=0, tiled=True)
    present = (requested >= 0).reshape(1, -1, 1)
    clamped = jnp.maximum(requested, 0).reshape(-1)
    chosen = jnp.where(present, jnp.take(box_dens, clamped, axis=1), 0.0)
    outgoing = chosen.reshape(S, ndev, CAP * R)
    received = lax.all_to_all(
        outgoing, ("row", "col"), split_axis=1, concat_axis=1, tiled=True
    ).reshape(S, ndev * CAP, R)
    source_pool = jnp.concatenate([box_dens, received], axis=1)
    ref_rank = slot_rank.reshape(-1)[v_source]
    position = jnp.where(owners == device, local_idx, box_count + owners * CAP + ref_rank)

    def one_box(source_pos, classes):
        sources = jnp.take(source_pool, source_pos, axis=1)
        tile_set = build_tiles(classes)
        return jnp.einsum("kij,jkr->ir", tile_set, sources, precision=highest)

    def box_group(pair):
        return jax.vmap(one_box)(pair[0], pair[1])

    result = lax.map(
        box_group, (position.reshape(box_count // 4, 4, VL), v_class.reshape(box_count // 4, 4, VL))
    )
    result = result.reshape(box_count, S, R)
    far_field = jnp.transpose(result, (1, 0, 2)).reshape(S, -1)
    return (coarse_part, far_field)


def solution(mesh):
    placed = (P(None, ("row", "col")), P(), P(("row", "col"), None), P(("row", "col"), None))
    return jax.shard_map(
        body,
        mesh=mesh,
        in_specs=placed,
        out_specs=(P(None, ("row", "col")), P(None, ("row", "col"))),
        check_vma=False,
    )
```

profile of v0, /device:TPU:0, one launch (start us, length us, event | category | flops | bytes accessed | tf_op | source)
XLA Modules:
  0.0 437.9 jit_solution(1824470420439124816)
XLA Ops:
  0.6 0.8 eq.58
  1.4 0.2 fusion.51
  1.8 0.2 reduce_window_sum.11
  2.2 0.7 copy.44
  2.9 7.3 %all-to-all-start = ((s32[32,1,2]{2,1,0:T(1,128)}), s32[32,1,2]{2,1,0:T(1,128)S(1)}, u32[]{:S(2)}, u32[]{:S(2)}) async-start(s32[32,1,2]{2,1,0:T(1,128)} %copy.44), calls=%async_computation | async-start | bytes 32768 | tf_op jit(solution)/shard_map/all_to_all | solution.py:97
  10.2 11.6 %copy.41 = f32[296,8192]{0,1:T(8,128)} copy(f32[296,8192]{1,0:T(8,128)} %param.10) | data formatting | bytes 19398656 | tf_op args[0]
  21.8 22.6 %fusion.43 = f32[296,16,64]{0,2,1:T(8,128)S(1)} fusion(f32[296,16,8,64]{0,3,2,1:T(8,128)} %bitcast.96, f32[8,296,296]{2,1,0:T(8,128)} %param.11), kind=kOutput, calls=%fused_computation.52 | convolution fusion | flops 8613003264 | bytes 13715456 | tf_op jit(solution)/shard_map/cij,jbcr->ibr/dot_general | solution.py:64
  44.8 3.6 gather_fusion.2
  48.4 6.2 %copy.50 = f32[296,32,128]{2,0,1:T(8,128)} copy(f32[296,32,128]{0,2,1:T(8,128)} %bitcast.97) | data formatting | bytes 9699328 | tf_op jit(solution)/shard_map/jit(_take)/gather | solution.py:100
  55.1 5.5 %select_select_fusion = f32[296,32,128]{2,0,1:T(8,128)} fusion(f32[296,32,128]{2,0,1:T(8,128)} %copy.50, pred[32,128]{1,0:T(8,128)(4,1)S(1)} %broadcast_in_dim.78, pred[32,128]{1,0:T(8,128)(4,1)S(1)} %broadcast_in_dim.75), kind=kLoop, calls=%fused_computation.44 | loop fusion | flops 2424832 | bytes 9707520 | tf_op jit(solution)/shard_map/jit(_where)/select_n | solution.py:100
  60.7 6.1 %all-to-all-start.1 = ((f32[296,32,128]{2,0,1:T(8,128)}), f32[296,32,128]{2,0,1:T(8,128)}, u32[]{:S(2)}, u32[]{:S(2)}) async-start(f32[296,32,128]{2,0,1:T(8,128)} %select_select_fusion), calls=%async_computation.1 | async-start | bytes 9699328 | tf_op jit(solution)/shard_map/all_to_all | solution.py:102
  66.9 6.0 %gather_fusion.4 = f32[16,296,296]{2,1,0:T(8,128)} fusion(f32[8,296,296]{2,1,0:T(8,128)} %param.11, s32[1024]{0:T(1024)S(1)} %pad_clamp_fusion.3), kind=kCustom, calls=%fused_computation.2.clone | custom fusion | bytes 11214912 | tf_op jit(solution)/shard_map/jit(_take)/gather | solution.py:71
  72.9 6.0 %gather_fusion.3 = f32[16,296,296]{2,1,0:T(8,128)} fusion(f32[8,296,296]{2,1,0:T(8,128)} %param.11, s32[1024]{0:T(1024)S(1)} %pad_clamp_fusion.4), kind=kCustom, calls=%fused_computation.clone | custom fusion | bytes 11214912 | tf_op jit(solution)/shard_map/jit(_take)/gather | solution.py:74
  78.9 9.9 %fusion.32 = f32[16,64,296]{2,1,0:T(8,128)S(1)} fusion(f32[296,16,64]{0,2,1:T(8,128)S(1)} %fusion.43, f32[16,296,296]{2,1,0:T(8,128)} %gather_fusion.4, pred[16]{0:T(512)(128)(4,1)S(1)} %get-tuple-element.90), kind=kOutput, calls=%fused_computation.40 | convolution fusion | flops 1078027264 | bytes 8032272 | tf_op jit(solution)/shard_map/bij,jbr->ibr/dot_general | solution.py:70
  88.9 7.2 %fusion.46 = f32[296,64]{0,1:T(8,128)S(1)} fusion(f32[16,64,296]{2,1,0:T(8,128)S(1)} %fusion.32, f32[16,296,296]{2,1,0:T(8,128)S(1)} %copy-done, pred[16]{0:T(512)(128)(4,1)S(1)} %get-tuple-element.91), kind=kOutput, calls=%fused_computation.53 | convolution fusion | flops 1078027264 | bytes 6895632 | tf_op jit(solution)/shard_map/bij,jbr->ir/dot_general | solution.py:73
  96.3 2.8 gather_fusion.1
  99.3 1.7 collective-permute-start.1
  101.0 3.8 collective-permute-done.1
  104.8 0.6 dynamic-slice_add_fusion
  105.4 69.2 %all-to-all-done.1 = f32[296,32,128]{2,0,1:T(8,128)} async-done(((f32[296,32,128]{2,0,1:T(8,128)}), f32[296,32,128]{2,0,1:T(8,128)}, u32[]{:S(2)}, u32[]{:S(2)}) %all-to-all-start.1) | async-done | bytes 4849696 | tf_op jit(solution)/shard_map/all_to_all | solution.py:102
  174.7 6.3 %copy.51 = f32[296,32,128]{0,2,1:T(8,128)} copy(f32[296,32,128]{2,0,1:T(8,128)} %all-to-all-done.1) | data formatting | bytes 9699328 | tf_op jit(solution)/shard_map/all_to_all | solution.py:102
  181.0 7.0 %pad_maximum_fusion = f32[296,80,64]{0,2,1:T(8,128)} fusion(f32[296,64,64]{0,2,1:T(8,128)} %bitcast.98, f32[296,16,64]{0,2,1:T(8,128)S(1)} %fusion.43), kind=kLoop, calls=%fused_computation.39 | loop fusion | flops 1515520 | bytes 12124160 | tf_op jit(solution)/shard_map/concatenate | solution.py:105
  188.0 248.4 %while.11 = (s32[]{:T(128)}, f32[4,4,296,64]{2,3,1,0:T(8,128)S(1)}, s32[4,4,22]{2,1,0:T(4,128)}, s32[4,4,22]{2,1,0:T(4,128)S(1)}, f32[296,80,64]{0,2,1:T(8,128)}...) while((s32[]{:T(128)}, f32[4,4,296,64]{2,3,1,0:T(8,128)S(1)}, ...), condition=%wide.region_5.7_spmd.clone, body=%wide.region_4.6_spmd.sunk.clone.sunk | while | flops 5993607680 | bytes 36497716 | solution.py:117
  188.2 0.7 dynamic-slice_bitcast_fusion.2
  188.9 0.4 fusion.82
  189.3 0.1 broadcast_subtract_fusion.5
  189.6 7.7 %gather_fusion = f32[88,296,64]{1,2,0:T(8,128)} fusion(f32[296,80,64]{0,2,1:T(8,128)} %get-tuple-element.163, s32[1024]{0:T(1024)S(1)} %pad_clamp_fusion.6), kind=kCustom, calls=%fused_computation.1.clone.1 | custom fusion | bytes 13336928 | tf_op jit(solution)/shard_map/while/body/eval_jaxpr/vmap(jit(_take))/gather | solution.py:110
  197.3 4.6 %fusion.84 = f32[4,296,22,64]{1,3,2,0:T(8,128)S(1)} fusion(f32[4,22,296,64]{2,3,1,0:T(8,128)} %bitcast.95, pred[4,22]{1,0:T(4,128)(4,1)S(1)} %compare_and_fusion.4), kind=kLoop, calls=%fused_computation.20.clone.clone.clone.clone.clone.2.clone.1 | loop fusion | flops 1667072 | bytes 13336664 | tf_op jit(solution)/shard_map/while/body/eval_jaxpr/vmap(kij,jkr->ir)/dot_general | solution.py:112
  202.0 48.3 %fusion.85 = f32[4,4,296,64]{2,3,1,0:T(8,128)S(1)} fusion(f32[4,4,296,64]{2,3,1,0:T(8,128)S(1)} %get-tuple-element.147, s32[]{:T(128)S(6)} %copy.58, f32[296]{0:T(512)S(1)} %get-tuple-element.165, f32[296]{0:T(512)S(1)} %get-tuple-element.166, f32[296]{0:T(512)S(1)} %get-tuple-element.167, f32[4,22,296]{2,1,0:T(8,128)S(1)} %get-tuple-element.130, ...), kind=kOutput, calls=%fused_computation.25.clone.3 | convolution fusion | flops 5990831616 | bytes 9492484 | tf_op jit(solution)/shard_map/while/body/eval_jaxpr/vmap(kij,jkr->ir)/dot_general | solution.py:112
  250.3 0.7 dynamic-slice_bitcast_fusion.2
  250.9 0.4 fusion.82
  251.4 0.1 broadcast_subtract_fusion.5
  251.7 7.7 %gather_fusion = f32[88,296,64]{1,2,0:T(8,128)} fusion(f32[296,80,64]{0,2,1:T(8,128)} %get-tuple-element.163, s32[1024]{0:T(1024)S(1)} %pad_clamp_fusion.6), kind=kCustom, calls=%fused_computation.1.clone.1 | custom fusion | bytes 13336928 | tf_op jit(solution)/shard_map/while/body/eval_jaxpr/vmap(jit(_take))/gather | solution.py:110
  259.4 4.6 %fusion.84 = f32[4,296,22,64]{1,3,2,0:T(8,128)S(1)} fusion(f32[4,22,296,64]{2,3,1,0:T(8,128)} %bitcast.95, pred[4,22]{1,0:T(4,128)(4,1)S(1)} %compare_and_fusion.4), kind=kLoop, calls=%fused_computation.20.clone.clone.clone.clone.clone.2.clone.1 | loop fusion | flops 1667072 | bytes 13336664 | tf_op jit(solution)/shard_map/while/body/eval_jaxpr/vmap(kij,jkr->ir)/dot_general | solution.py:112
  264.0 48.3 %fusion.85 = f32[4,4,296,64]{2,3,1,0:T(8,128)S(1)} fusion(f32[4,4,296,64]{2,3,1,0:T(8,128)S(1)} %get-tuple-element.147, s32[]{:T(128)S(6)} %copy.58, f32[296]{0:T(512)S(1)} %get-tuple-element.165, f32[296]{0:T(512)S(1)} %get-tuple-element.166, f32[296]{0:T(512)S(1)} %get-tuple-element.167, f32[4,22,296]{2,1,0:T(8,128)S(1)} %get-tuple-element.130, ...), kind=kOutput, calls=%fused_computation.25.clone.3 | convolution fusion | flops 5990831616 | bytes 9492484 | tf_op jit(solution)/shard_map/while/body/eval_jaxpr/vmap(kij,jkr->ir)/dot_general | solution.py:112
  312.3 0.7 dynamic-slice_bitcast_fusion.2
  313.0 0.4 fusion.82
  313.4 0.1 broadcast_subtract_fusion.5
  313.7 7.7 %gather_fusion = f32[88,296,64]{1,2,0:T(8,128)} fusion(f32[296,80,64]{0,2,1:T(8,128)} %get-tuple-element.163, s32[1024]{0:T(1024)S(1)} %pad_clamp_fusion.6), kind=kCustom, calls=%fused_computation.1.clone.1 | custom fusion | bytes 13336928 | tf_op jit(solution)/shard_map/while/body/eval_jaxpr/vmap(jit(_take))/gather | solution.py:110
  321.4 4.6 %fusion.84 = f32[4,296,22,64]{1,3,2,0:T(8,128)S(1)} fusion(f32[4,22,296,64]{2,3,1,0:T(8,128)} %bitcast.95, pred[4,22]{1,0:T(4,128)(4,1)S(1)} %compare_and_fusion.4), kind=kLoop, calls=%fused_computation.20.clone.clone.clone.clone.clone.2.clone.1 | loop fusion | flops 1667072 | bytes 13336664 | tf_op jit(solution)/shard_map/while/body/eval_jaxpr/vmap(kij,jkr->ir)/dot_general | solution.py:112
  326.1 48.3 %fusion.85 = f32[4,4,296,64]{2,3,1,0:T(8,128)S(1)} fusion(f32[4,4,296,64]{2,3,1,0:T(8,128)S(1)} %get-tuple-element.147, s32[]{:T(128)S(6)} %copy.58, f32[296]{0:T(512)S(1)} %get-tuple-element.165, f32[296]{0:T(512)S(1)} %get-tuple-element.166, f32[296]{0:T(512)S(1)} %get-tuple-element.167, f32[4,22,296]{2,1,0:T(8,128)S(1)} %get-tuple-element.130, ...), kind=kOutput, calls=%fused_computation.25.clone.3 | convolution fusion | flops 5990831616 | bytes 9492484 | tf_op jit(solution)/shard_map/while/body/eval_jaxpr/vmap(kij,jkr->ir)/dot_general | solution.py:112
  374.4 0.7 dynamic-slice_bitcast_fusion.2
  375.0 0.4 fusion.82
  375.5 0.1 broadcast_subtract_fusion.5
  375.8 7.7 %gather_fusion = f32[88,296,64]{1,2,0:T(8,128)} fusion(f32[296,80,64]{0,2,1:T(8,128)} %get-tuple-element.163, s32[1024]{0:T(1024)S(1)} %pad_clamp_fusion.6), kind=kCustom, calls=%fused_computation.1.clone.1 | custom fusion | bytes 13336928 | tf_op jit(solution)/shard_map/while/body/eval_jaxpr/vmap(jit(_take))/gather | solution.py:110
  383.5 4.6 %fusion.84 = f32[4,296,22,64]{1,3,2,0:T(8,128)S(1)} fusion(f32[4,22,296,64]{2,3,1,0:T(8,128)} %bitcast.95, pred[4,22]{1,0:T(4,128)(4,1)S(1)} %compare_and_fusion.4), kind=kLoop, calls=%fused_computation.20.clone.clone.clone.clone.clone.2.clone.1 | loop fusion | flops 1667072 | bytes 13336664 | tf_op jit(solution)/shard_map/while/body/eval_jaxpr/vmap(kij,jkr->ir)/dot_general | solution.py:112
  388.1 48.3 %fusion.85 = f32[4,4,296,64]{2,3,1,0:T(8,128)S(1)} fusion(f32[4,4,296,64]{2,3,1,0:T(8,128)S(1)} %get-tuple-element.147, s32[]{:T(128)S(6)} %copy.58, f32[296]{0:T(512)S(1)} %get-tuple-element.165, f32[296]{0:T(512)S(1)} %get-tuple-element.166, f32[296]{0:T(512)S(1)} %get-tuple-element.167, f32[4,22,296]{2,1,0:T(8,128)S(1)} %get-tuple-element.130, ...), kind=kOutput, calls=%fused_computation.25.clone.3 | convolution fusion | flops 5990831616 | bytes 9492484 | tf_op jit(solution)/shard_map/while/body/eval_jaxpr/vmap(kij,jkr->ir)/dot_general | solution.py:112
  436.4 1.5 copy.52
  (78 shorter events, 2.5 us)
Async XLA Ops:
  2.9 41.6 %all-to-all-start = ((s32[32,1,2]{2,1,0:T(1,128)}), s32[32,1,2]{2,1,0:T(1,128)S(1)}, u32[]{:S(2)}, u32[]{:S(2)}) async-start(s32[32,1,2]{2,1,0:T(1,128)} %copy.44), calls=%async_computation | async-start | bytes 32768 | tf_op jit(solution)/shard_map/all_to_all | solution.py:97
  60.7 114.0 %all-to-all-start.1 = ((f32[296,32,128]{2,0,1:T(8,128)}), f32[296,32,128]{2,0,1:T(8,128)}, u32[]{:S(2)}, u32[]{:S(2)}) async-start(f32[296,32,128]{2,0,1:T(8,128)} %select_select_fusion), calls=%async_computation.1 | async-start | bytes 9699328 | tf_op jit(solution)/shard_map/all_to_all | solution.py:102
  78.9 10.0 %copy-start = (f32[16,296,296]{2,1,0:T(8,128)S(1)}, f32[16,296,296]{2,1,0:T(8,128)}, u32[]{:S(2)}) copy-start(f32[16,296,296]{2,1,0:T(8,128)} %gather_fusion.3) | copy-start | bytes 16822276
  88.8 7.4 %copy-start.1 = (s32[16,22]{1,0:T(8,128)S(1)}, s32[16,22]{1,0:T(8,128)}, u32[]{:S(2)}) copy-start(s32[16,22]{1,0:T(8,128)} %param.12) | copy-start | bytes 4228
  96.0 3.2 collective-permute-start
  99.3 5.6 %collective-permute-start.1 = (f32[296,64]{0,1:T(8,128)S(1)}, f32[296,64]{0,1:T(8,128)S(1)}, u32[]{:S(2)}, u32[]{:S(2)}) collective-permute-start(f32[296,64]{0,1:T(8,128)S(1)} %add.105), channel_id=1, source_target_pairs={{0,2},{1,3},{2,0},{3,1},{4,6},{5,7},{6,4},{7,5},{8,10},{9,11},{10,... | collective-permute-start | bytes 227336 | tf_op jit(solution)/shard_map/ppermute | solution.py:24
  180.9 7.0 %copy-start.2 = (f32[296]{0:T(512)S(1)}, f32[296]{0:T(512)}, u32[]{:S(2)}) copy-start(f32[296]{0:T(512)} %constant.263) | copy-start | bytes 3556
  180.9 7.0 %copy-start.3 = (f32[296]{0:T(512)S(1)}, f32[296]{0:T(512)}, u32[]{:S(2)}) copy-start(f32[296]{0:T(512)} %constant.264) | copy-start | bytes 3556
  180.9 7.0 %copy-start.4 = (f32[296]{0:T(512)S(1)}, f32[296]{0:T(512)}, u32[]{:S(2)}) copy-start(f32[296]{0:T(512)} %constant.265) | copy-start | bytes 3556
  180.9 7.0 %copy-start.5 = (f32[316,3,1]{0,1,2:T(4,128)S(1)}, f32[316,3,1]{0,1,2:T(4,128)}, u32[]{:S(2)}) copy-start(f32[316,3,1]{0,1,2:T(4,128)} %constant.262) | copy-start | bytes 11380
  180.9 7.0 %copy-start.6 = (f32[296]{0:T(512)S(1)}, f32[296]{0:T(512)}, u32[]{:S(2)}) copy-start(f32[296]{0:T(512)} %constant.259) | copy-start | bytes 3556
  180.9 7.0 %copy-start.7 = (f32[296]{0:T(512)S(1)}, f32[296]{0:T(512)}, u32[]{:S(2)}) copy-start(f32[296]{0:T(512)} %constant.260) | copy-start | bytes 3556
  180.9 7.0 %copy-start.8 = (f32[296]{0:T(512)S(1)}, f32[296]{0:T(512)}, u32[]{:S(2)}) copy-start(f32[296]{0:T(512)} %constant.261) | copy-start | bytes 3556
where the time goes:
time: 439 us; the launch traced here: 438 us
  matrix products  234 us (53%)
  local copies, waits for them, and re-layouts  80.6 us (18%)
  waiting for transfers between devices  73 us (17%)
  other arithmetic  33.2 us (8%)
  starting transfers between devices  15.2 us (3%)
    dot_general x4, matrix products, one_box(): return jnp.einsum('kij,jkr->ir', tile_set, sources, precision=highest)  193 us
    all_to_all x1, waiting for transfers between devices, body(): lax.all_to_all(outgoing, ('row', 'col'), split_axis=1, concat_axis=1, til...  69.2 us
    gather x4, local copies, waits for them, and re-layouts, one_box(): sources = jnp.take(source_pool, source_pos, axis=1)  30.8 us
    dot_general x1, matrix products, body(): box_dens = jnp.einsum('cij,jbcr->ibr', m2m, leaves, precision=highest)  22.6 us
    dot_general x4, other arithmetic, one_box(): return jnp.einsum('kij,jkr->ir', tile_set, sources, precision=highest)  18.5 us
    unnamed x20, local copies, waits for them, and re-layouts  13.1 us
    dot_general x1, matrix products, body(): jnp.einsum('bij,jbr->ibr', jnp.take(m2m, first_pos, axis=0), box_dens, pr...  9.93 us
    gather x2, local copies, waits for them, and re-layouts, body(): chosen = jnp.where(present, jnp.take(box_dens, clamped, axis=1), 0.0)  9.8 us
  transfers between devices with their start and end apart: 4, of which 2 were waited for; matrix products, arithmetic and copies ran while one was open for 15% of the time, Pallas kernels for 0%

commit v1 on v0

v1 whole, which is shorter than its diff:
```python
import functools
import math

import jax
import jax.numpy as jnp
import numpy as np
from jax import lax
from jax.experimental import pallas as pl
from jax.experimental.pallas import tpu as pltpu
from jax.sharding import PartitionSpec as P

CAP = 2
LANES = 128
KPAD = 384

radius = 0.525
kernel_scale = 1.0 / (4.0 * math.pi)
bf16 = jnp.bfloat16
f32 = jnp.float32


def surface_points(count):
    edge_count = 2
    while edge_count**3 - (edge_count - 2) ** 3 != count:
        edge_count += 1
    coords = np.linspace(-1.0, 1.0, edge_count)
    lattice = np.stack(np.meshgrid(coords, coords, coords, indexing="ij"), -1).reshape(-1, 3)
    border = np.max(np.abs(lattice), axis=1) > 1.0 - 1e-09
    return lattice[border]


def offset_table():
    coords = np.arange(-3, 4)
    lattice = np.stack(np.meshgrid(coords, coords, coords, indexing="ij"), -1).reshape(-1, 3)
    farther = np.max(np.abs(lattice), axis=1) >= 2
    return lattice[farther]


def low_lanes(rows):
    return lax.broadcasted_iota(jnp.int32, (rows, LANES), 1) < LANES // 2


def half_turn(value):
    return pltpu.roll(value, LANES // 2, 1)


def row_tiles(count):
    return [(start, min(16, count - start)) for start in range(0, count, 16)]


def split_store(value, rows, hi_ref, lo_ref, at_row, at_lane, lanes):
    hi = value.astype(bf16)
    lo = (value - hi.astype(f32)).astype(bf16)
    hi_ref[at_row : at_row + rows, at_lane : at_lane + lanes] = hi
    lo_ref[at_row : at_row + rows, at_lane : at_lane + lanes] = lo


def pair_columns(first, second, rows):
    low = low_lanes(rows)
    return (
        jnp.where(low, first, half_turn(second)),
        jnp.where(low, half_turn(first), second),
    )


def three_dots(m_hi, m_lo, x_hi, x_lo):
    out = jnp.dot(m_hi, x_hi, preferred_element_type=f32)
    out = out + jnp.dot(m_lo, x_hi, preferred_element_type=f32)
    return out + jnp.dot(m_hi, x_lo, preferred_element_type=f32)


def upward_kernel(leaf_ref, m_ref, out_ref, mh_ref, ml_ref, xh, xl):
    size = m_ref.shape[1]

    @pl.when(pl.program_id(0) == 0)
    def _():
        mh_ref[...] = jnp.zeros_like(mh_ref)
        ml_ref[...] = jnp.zeros_like(ml_ref)
        xh[...] = jnp.zeros_like(xh)
        xl[...] = jnp.zeros_like(xl)
        for child in range(8):
            for start, rows in row_tiles(size):
                split_store(
                    m_ref[child, start : start + rows, :], rows, mh_ref, ml_ref, start, child * KPAD, size
                )

    for slab in range(out_ref.shape[0]):
        for duo in range(4):
            left = slab * 8 * LANES + duo * LANES
            right = left + 4 * LANES
            for start, rows in row_tiles(size):
                even, odd = pair_columns(
                    leaf_ref[start : start + rows, left : left + LANES],
                    leaf_ref[start : start + rows, right : right + LANES],
                    rows,
                )
                split_store(even, rows, xh, xl, 2 * duo * KPAD + start, slab * LANES, LANES)
                split_store(odd, rows, xh, xl, (2 * duo + 1) * KPAD + start, slab * LANES, LANES)
    out = three_dots(mh_ref[...], ml_ref[...], xh[...], xl[...])
    for slab in range(out_ref.shape[0]):
        out_ref[slab] = out[:, slab * LANES : (slab + 1) * LANES]


def upward(leaf, m2m, slabs):
    size = m2m.shape[1]
    step = 2
    return pl.pallas_call(
        upward_kernel,
        grid=(slabs // step,),
        in_specs=[
            pl.BlockSpec((size, step * 8 * LANES), lambda i: (0, i)),
            pl.BlockSpec(m2m.shape, lambda i: (0, 0, 0)),
        ],
        out_specs=[
            pl.BlockSpec((step, size, LANES), lambda i: (i, 0, 0)),
            pl.BlockSpec((size, 8 * KPAD), lambda i: (0, 0)),
            pl.BlockSpec((size, 8 * KPAD), lambda i: (0, 0)),
        ],
        out_shape=[
            jax.ShapeDtypeStruct((slabs, size, LANES), f32),
            jax.ShapeDtypeStruct((size, 8 * KPAD), bf16),
            jax.ShapeDtypeStruct((size, 8 * KPAD), bf16),
        ],
        scratch_shapes=[
            pltpu.VMEM((8 * KPAD, step * LANES), bf16),
            pltpu.VMEM((8 * KPAD, step * LANES), bf16),
        ],
        cost_estimate=pl.CostEstimate(
            flops=2 * 8 * size * size * slabs * LANES * 3,
            bytes_accessed=4 * (leaf.size + m2m.size),
            transcendentals=0,
        ),
        name="upward",
    )(leaf, m2m)


def coarse_kernel(first_ref, pool_ref, mh_ref, ml_ref, out_ref, xh, xl, yh, yl):
    size = out_ref.shape[0]
    for ref in (xh, xl, yh, yl):
        ref[...] = jnp.zeros_like(ref)
    for duo in range(4):
        for start, rows in row_tiles(size):
            even, odd = pair_columns(
                pool_ref[duo, start : start + rows, :], pool_ref[4 + duo, start : start + rows, :], rows
            )
            split_store(even, rows, xh, xl, 2 * duo * KPAD + start, 0, LANES)
            split_store(odd, rows, xh, xl, (2 * duo + 1) * KPAD + start, 0, LANES)
    upper = three_dots(mh_ref[...], ml_ref[...], xh[...], xl[...])
    for start, rows in row_tiles(size):
        part = upper[start : start + rows]
        low = low_lanes(rows)
        split_store(jnp.where(low, part, 0.0), rows, yh, yl, start, 0, LANES)
        split_store(jnp.where(low, half_turn(part), 0.0), rows, yh, yl, KPAD + start, 0, LANES)
    at = pl.multiple_of(first_ref[0] * KPAD, LANES)
    out = three_dots(
        mh_ref[:, pl.ds(at, 2 * KPAD)], ml_ref[:, pl.ds(at, 2 * KPAD)], yh[...], yl[...]
    )
    out_ref[...] = out[:, : out_ref.shape[1]]


def coarse_partial(pool, mh, ml, first, rhs):
    slabs, size, _ = pool.shape
    vmem = pl.BlockSpec(memory_space=pltpu.VMEM)
    return pl.pallas_call(
        coarse_kernel,
        in_specs=[pl.BlockSpec(memory_space=pltpu.SMEM), vmem, vmem, vmem],
        out_specs=vmem,
        out_shape=jax.ShapeDtypeStruct((size, rhs), f32),
        scratch_shapes=[
            pltpu.VMEM((8 * KPAD, LANES), bf16),
            pltpu.VMEM((8 * KPAD, LANES), bf16),
            pltpu.VMEM((2 * KPAD, LANES), bf16),
            pltpu.VMEM((2 * KPAD, LANES), bf16),
        ],
        cost_estimate=pl.CostEstimate(
            flops=2 * 8 * size * size * 2 * LANES * 3,
            bytes_accessed=4 * pool.size + 4 * mh.size,
            transcendentals=0,
        ),
        name="coarse",
    )(first, pool, mh, ml)


def fold_rows(size):
    first = size // 2 // 16 * 16
    return first, size - first


def choose_kernel(count, slot, wanted_ref, pool_ref, out_ref, ready, sems):
    size = pool_ref.shape[1]
    upper, lower = fold_rows(size)

    def send(dest):
        return pltpu.make_async_copy(ready.at[dest], out_ref.at[dest], sems.at[dest])

    @pl.loop(0, count)
    def _(dest):
        box = wanted_ref[CAP * dest + slot]
        slab = lax.shift_right_logical(box, 1)
        odd = (box & 1) == 1
        for start, rows in row_tiles(lower):
            under = pool_ref[slab, upper + start : upper + start + rows, :]
            under = jnp.where(odd, under, half_turn(under))
            have = min(rows, upper - start)
            if have <= 0:
                over = jnp.zeros_like(under)
            else:
                over = pool_ref[slab, start : start + have, :]
                over = jnp.where(odd, half_turn(over), over)
                if have < rows:
                    over = jnp.concatenate([over, jnp.zeros((rows - have, LANES), f32)], axis=0)
            ready[dest, start : start + rows, :] = jnp.where(low_lanes(rows), over, under)
        send(dest).start()

    for dest in range(count):
        send(dest).wait()


def choose(pool, wanted, slot, after):
    dests = wanted.shape[0]
    size = pool.shape[1]
    shape = (dests, fold_rows(size)[1], LANES)
    return pl.pallas_call(
        functools.partial(choose_kernel, dests, slot),
        in_specs=[pl.BlockSpec(memory_space=pltpu.SMEM), pl.BlockSpec(memory_space=pltpu.VMEM)],
        out_specs=pl.BlockSpec(memory_space=pl.ANY),
        out_shape=jax.ShapeDtypeStruct(shape, f32),
        scratch_shapes=[pltpu.VMEM(shape, f32), pltpu.SemaphoreType.DMA((dests,))],
        cost_estimate=pl.CostEstimate(
            flops=0, bytes_accessed=4 * (pool.size + math.prod(shape)), transcendentals=0
        ),
        name="choose",
    )(tie(wanted.reshape(-1), after), pool)


def tie(value, after):
    return value if after is None else lax.optimization_barrier((value, after))[0]


MAIN = 256
TAIL = 64


def field_kernel(first, last, boxes, size, tbl_ref, list_ref, span_ref, col_ref, row_ref, pool_ref, *rest):
    rest = list(rest)
    acc_in = None if first else rest.pop(0)
    out_ref, sp, dist = rest[:3]
    rest = rest[3:]
    acc = rest.pop(0) if last else out_ref
    slabs, held, _ = pool_ref.shape
    upper, lower = fold_rows(size)
    folded = held != size
    rows_pad = dist.shape[0]
    if first:
        acc[...] = jnp.zeros_like(acc)
    else:
        carried = pltpu.make_async_copy(acc_in, acc, rest.pop(0))
        carried.start()

    for start, rows in row_tiles(rows_pad):
        for lane in range(0, KPAD, LANES):
            total = jnp.zeros((rows, LANES), f32)
            for comp in range(3):
                delta = (
                    col_ref[comp, start : start + rows, :] - row_ref[comp : comp + 1, lane : lane + LANES]
                )
                total = total + delta * delta
            dist[start : start + rows, lane : lane + LANES] = total

    @pl.loop(0, slabs)
    def _(slab):
        def keep(source, at, value):
            lesser = value - value.astype(bf16).astype(f32)
            sp[source, at : at + value.shape[0], :] = jnp.where(
                low_lanes(value.shape[0]), value, lesser
            ).astype(bf16)

        def empty(source, at):
            rows = MAIN + TAIL - at
            sp[source, at : at + rows, :] = jnp.zeros((rows, LANES), bf16)

        for start, rows in row_tiles(held):
            value = pool_ref[slab, start : start + rows, :]
            if rows < 16:
                value = jnp.concatenate([value, jnp.zeros((16 - rows, LANES), f32)], axis=0)
            low = low_lanes(16)
            turned = half_turn(value)
            left, right = jnp.where(low, value, turned), jnp.where(low, turned, value)
            if folded:
                if start < upper:
                    keep(slab, start, left)
                keep(slab, upper + start, right)
            else:
                keep(2 * slab, start, left)
                keep(2 * slab + 1, start, right)
        ending = -(-size // 16) * 16
        for source in (slab,) if folded else (2 * slab, 2 * slab + 1):
            empty(source, ending)

    if not first:
        carried.wait()
    begin = span_ref[0]
    count = span_ref[1]

    def read(index):
        code = list_ref[begin + jnp.minimum(index, count - 1)]
        cls = lax.shift_right_logical(code, 12)
        source = code & 255
        target = jnp.where(index < count, lax.shift_right_logical(code, 8) & 15, boxes)
        return [tbl_ref[cls * 3 + comp] for comp in range(3)], source, target

    def duo(index, sums):
        members = [read(index), read(index + 1)]
        shifts, twice = [], []
        for offset, _, _ in members:
            base = offset[0] * offset[0] + offset[1] * offset[1] + offset[2] * offset[2]
            double = [2.0 * comp for comp in offset]
            twice.append(double)
            shifts.append(
                double[0] * row_ref[0:1, :] + double[1] * row_ref[1:2, :] + double[2] * row_ref[2:3, :] + base
            )
        low = low_lanes(16)
        shift_tail = jnp.where(low[:1], shifts[0][:, MAIN:], shifts[1][:, MAIN:])
        tiles = []
        for start, rows in row_tiles(rows_pad):
            point = [col_ref[comp, start : start + rows, :] for comp in range(3)]
            owns = [d[0] * point[0] + d[1] * point[1] + d[2] * point[2] for d in twice]
            parts = []
            for own, shift in zip(owns, shifts):
                own = jnp.concatenate([own, own], axis=1)
                value = lax.rsqrt(dist[start : start + rows, :MAIN] + (shift[:, :MAIN] - own))
                hi = value.astype(bf16)
                parts += [hi, (value - hi.astype(f32)).astype(bf16)]
            own = jnp.where(low, owns[0], owns[1])
            value = lax.rsqrt(dist[start : start + rows, MAIN:] + (shift_tail - own))
            hi = value.astype(bf16)
            parts.append(jnp.concatenate([hi, (value - hi.astype(f32)).astype(bf16)], axis=1))
            tiles.append(parts)

        mains, tails = [], []
        for at, (_, source, _) in enumerate(members):
            for begin_row, rows, kept in ((0, MAIN, mains), (MAIN, TAIL, tails)):
                part = sp[source, begin_row : begin_row + rows, :]
                empty = jnp.zeros_like(part)
                kept.append(jnp.concatenate([part, empty] if at == 0 else [empty, part], axis=1))
        stationary = [mains[0], mains[0], mains[1], mains[1], jnp.concatenate(tails * 2, axis=0)]
        for chunk, rhs in enumerate(stationary):
            fresh = chunk not in (1, 3)
            for unit in range(2):
                if fresh:
                    pltpu.matmul_push_rhs(rhs, 0, unit)
                for at in range(unit, len(tiles), 2):
                    pltpu.matmul_acc_lhs(sums[at], tiles[at][chunk], 0 if at == unit and fresh else None)
        for at, (start, rows) in enumerate(row_tiles(rows_pad)):
            have = min(rows, size - start)
            product = pltpu.matmul_pop(sums[at])
            for number, (_, _, target) in enumerate(members):
                mine = product[:have, number * LANES : (number + 1) * LANES]
                acc[target, start : start + have, :] = acc[target, start : start + have, :] + mine

    def duos(*flat):
        sums = flat[: len(flat) // 2], flat[len(flat) // 2 :]

        whole = lax.shift_right_logical(count, 3)

        @pl.loop(0, whole)
        def _(step):
            for half in range(4):
                duo(8 * step + 2 * half, sums[half % 2])

        @pl.loop(4 * whole, lax.shift_right_logical(count + 1, 1))
        def _(step):
            duo(2 * step, sums[0])

    tiles_of = enumerate(row_tiles(rows_pad))
    kinds = [pltpu.ACC(at % 2)((rows, 256), f32) for at, (_, rows) in tiles_of]
    pl.run_scoped(duos, *kinds, *kinds)

    if last:
        for slab in range(boxes // 2):
            for start, rows in row_tiles(size):
                left = acc[2 * slab, start : start + rows, :]
                right = acc[2 * slab + 1, start : start + rows, :]
                out_ref[start : start + rows, slab * LANES : (slab + 1) * LANES] = kernel_scale * jnp.where(
                    low_lanes(rows), left + half_turn(left), right + half_turn(right)
                )


def field(pool, acc, listing, span, boxes, size, last, after):
    slabs, held, _ = pool.shape
    sources = slabs if held != size else 2 * slabs
    points = surface_points(size) * radius
    rows_pad = -(-size // 16) * 16
    col = np.zeros((3, rows_pad, LANES), np.float32)
    col[:, :size] = points.T[:, :, None]
    row = np.zeros((8, KPAD), np.float32)
    row[:3, :size] = points.T
    row[:, MAIN + TAIL :] = row[:, MAIN : MAIN + TAIL]
    vmem = pl.BlockSpec(memory_space=pltpu.VMEM)
    smem = pl.BlockSpec(memory_space=pltpu.SMEM)
    first = acc is None
    args = [jnp.asarray(offset_table().reshape(-1), f32), listing, tie(span, after), jnp.asarray(col), jnp.asarray(row), pool]
    specs = [smem, smem, smem, vmem, vmem, vmem]
    sums = (boxes + 1, size, LANES)
    scratch = [
        pltpu.VMEM((sources, MAIN + TAIL, LANES), bf16),
        pltpu.VMEM((rows_pad, KPAD), f32),
    ]
    if last:
        scratch.append(pltpu.VMEM(sums, f32))
    if not first:
        args.append(acc)
        specs.append(pl.BlockSpec(memory_space=pl.ANY))
        scratch.append(pltpu.SemaphoreType.DMA)
    pairs = listing.shape[0] // 3
    return pl.pallas_call(
        functools.partial(field_kernel, first, last, boxes, size),
        in_specs=specs,
        out_specs=vmem,
        out_shape=jax.ShapeDtypeStruct((size, boxes * LANES // 2) if last else sums, f32),
        scratch_shapes=scratch,
        compiler_params=pltpu.CompilerParams(vmem_limit_bytes=60 * 1024 * 1024),
        cost_estimate=pl.CostEstimate(
            flops=2 * rows_pad * 2 * KPAD * LANES * pairs,
            bytes_accessed=4 * pool.size,
            transcendentals=rows_pad * KPAD * pairs,
        ),
        name="field",
    )(*args)


def stage_lists(stage, codes, stages):
    slots = codes.shape[0]
    order = jnp.arange(slots, dtype=jnp.int32)
    ahead = (stage[None, :] < stage[:, None]) | (
        (stage[None, :] == stage[:, None]) & (order[None, :] < order[:, None])
    )
    place = jnp.sum(ahead.astype(jnp.int32), axis=1)
    listing = jnp.sum(jnp.where(place[None, :] == order[:, None], codes[None, :], 0), axis=1)
    numbers = jnp.arange(stages, dtype=jnp.int32)
    counts = jnp.sum((stage[None, :] == numbers[:, None]).astype(jnp.int32), axis=1)
    begins = jnp.sum((stage[None, :] < numbers[:, None]).astype(jnp.int32), axis=1)
    return listing, jnp.stack([begins, counts], axis=1)


def body(leaf_density, m2m, v_source, v_class):
    axes = ("row", "col")
    size = m2m.shape[1]
    box_count = v_source.shape[0]
    rhs = leaf_density.shape[1] // (8 * box_count)
    device, ndev = lax.axis_index(axes), lax.axis_size(axes)

    ids = v_source.reshape(-1)
    owner = ids // box_count
    named = ids[:, None] == jnp.arange(ndev * box_count, dtype=jnp.int32)[None, :]
    needed = jnp.any(named, axis=0).reshape(ndev, box_count)
    local = jnp.arange(box_count, dtype=jnp.int32)
    earlier = (local[None, :] < local[:, None])[None]
    rank = jnp.sum((needed[:, None, :] & earlier).astype(jnp.int32), axis=2)
    slots = jnp.arange(CAP, dtype=jnp.int32)
    hit = needed[:, None, :] & (rank[:, None, :] == slots[None, :, None])
    wanted = jnp.sum(jnp.where(hit, local[None, None, :], 0), axis=2)

    def exchange(value):
        return lax.all_to_all(value, axes, split_axis=0, concat_axis=0, tiled=True)

    requested = exchange(wanted)
    pool, mh, ml = upward(leaf_density, m2m, box_count // 2)
    chosen = choose(pool, requested, 0, None)
    received = exchange(chosen)

    pair_rank = jnp.sum(jnp.where(named, rank.reshape(-1)[None, :], 0), axis=1)
    mine = owner == device
    source = jnp.where(mine, ids % box_count, owner)
    target = jnp.repeat(jnp.arange(box_count, dtype=jnp.int32), v_source.shape[1])
    codes = v_class.reshape(-1) * 4096 + target * 256 + source
    listing, spans = stage_lists(jnp.where(mine, 0, 1 + pair_rank), codes, 1 + CAP)

    first = (device * (box_count // 8)) % 8
    current = coarse_partial(pool, mh, ml, tie(first.reshape(1).astype(jnp.int32), chosen), rhs)
    group_size = 64 // box_count
    for bit in range(group_size.bit_length() - 1):
        pairs = [(i, i ^ (1 << bit)) for i in range(ndev)]
        current = current + lax.ppermute(current, axes, pairs)
    share = rhs // group_size
    coarse = lax.dynamic_slice_in_dim(current, (device % group_size) * share, share, 1)

    chosen_second = choose(pool, requested, 1, chosen)
    acc = field(pool, None, listing, spans[0], box_count, size, False, chosen_second)
    received_second = exchange(tie(chosen_second, (received, acc, coarse)))
    acc = field(received, acc, listing, spans[1], box_count, size, False, None)
    out = field(received_second, acc, listing, spans[2], box_count, size, True, None)
    return (coarse, out)


def solution(mesh):
    both = ("row", "col")
    return jax.shard_map(
        body,
        mesh=mesh,
        in_specs=(P(None, both), P(), P(both, None), P(both, None)),
        out_specs=(P(None, both), P(None, both)),
        check_vma=False,
    )
```

time: 439 us -> 180 us (0.41)
  matrix products: 234 us -> 0 us
  Pallas kernels: 0 us -> 111 us
  local copies, waits for them, and re-layouts: 80.6 us -> 5.95 us
  waiting for transfers between devices: 73 us -> 40 us
  other arithmetic: 33.2 us -> 2.56 us
    dot_general x11 -> x0, matrix products: 234 us -> none  [the longest x4 193 us: one_box(): return jnp.einsum('kij,jkr->ir', tile_set, sources, precision=highest)]
    pallas_call x0 -> x7, Pallas kernels: none -> 111 us  [the longest x3 80.4 us: field(): pl.pallas_call(functools.partial(field_kernel, first, last, boxes, size),...]
    gather x10 -> x0, local copies, waits for them, and re-layouts: 55.4 us -> none  [the longest x4 30.8 us: one_box(): sources = jnp.take(source_pool, source_pos, axis=1)]
    all_to_all x2 -> x3, waiting for transfers between devices: 69.2 us -> 40 us  [exchange(): return lax.all_to_all(value, axes, split_axis=0, concat_axis=0, tiled=True)]
    dot_general x4 -> x0, other arithmetic: 18.5 us -> none  [one_box(): return jnp.einsum('kij,jkr->ir', tile_set, sources, precision=highest)]
    unnamed x20 -> x7, local copies, waits for them, and re-layouts: 13.1 us -> 2.15 us
    concatenate x1 -> x0, other arithmetic: 6.97 us -> none  [body(): source_pool = jnp.concatenate([box_dens, received], axis=1)]
    select_n x9 -> x1, other arithmetic: 5.64 us -> 0.01 us  [body(): jnp.where(mine, 0, 1 + pair_rank)]
  transfers between devices with their start and end apart: 4 -> 5, of which waited for: 2 -> 2; matrix products, arithmetic and copies ran while one was open for 15% -> 2% of each run, Pallas kernels for 0% -> 46%
where the time goes in v1:
time: 180 us
  Pallas kernels  111 us (62%)
  waiting for transfers between devices  40 us (22%)
  starting transfers between devices  19.3 us (11%)
  local copies, waits for them, and re-layouts  5.95 us (3%)
  other arithmetic  2.56 us (1%)
    pallas_call x3, Pallas kernels, field(): pl.pallas_call(functools.partial(field_kernel, first, last, boxes, size),...  80.4 us
    all_to_all x3, waiting for transfers between devices, exchange(): return lax.all_to_all(value, axes, split_axis=0, concat_axis=0, tiled=True)  40 us
    all_to_all x3, starting transfers between devices, exchange(): return lax.all_to_all(value, axes, split_axis=0, concat_axis=0, tiled=True)  17.4 us
    pallas_call x1, Pallas kernels, upward(): pl.pallas_call(upward_kernel, grid=(slabs // step,), in_specs=[pl.BlockSp...  12.8 us
    pallas_call x2, Pallas kernels, choose(): pl.pallas_call(functools.partial(choose_kernel, dests, slot), in_specs=[p...  11.5 us
    pallas_call x1, Pallas kernels, coarse_partial(): pl.pallas_call(coarse_kernel, in_specs=[pl.BlockSpec(memory_space=pltpu.S...  6.16 us
  transfers between devices with their start and end apart: 5, of which 2 were waited for; matrix products, arithmetic and copies ran while one was open for 2% of the time, Pallas kernels for 46%

profile of v1, /device:TPU:0, one launch (start us, length us, event | category | flops | bytes accessed | tf_op | source)
XLA Modules:
  0.0 179.6 jit_solution(14844635830144598840)
XLA Ops:
  0.6 0.8 eq.79
  1.4 0.2 fusion
  1.6 0.1 and.77
  1.7 0.1 copy.21
  1.8 0.1 convert_reduce_fusion.1
  1.9 0.7 copy.23
  2.6 7.3 %all-to-all-start = ((s32[32,1,2]{2,1,0:T(1,128)}), s32[32,1,2]{2,1,0:T(1,128)S(1)}, u32[]{:S(2)}, u32[]{:S(2)}) async-start(s32[32,1,2]{2,1,0:T(1,128)} %copy.23), calls=%async_computation | async-start | bytes 32768 | tf_op jit(solution)/shard_map/all_to_all | solution.py:465
  10.0 12.8 %upward.1 = (f32[8,296,128]{2,1,0:T(8,128)}, bf16[296,3072]{1,0:T(8,128)(2,1)}, bf16[296,3072]{1,0:T(8,128)(2,1)}) custom-call(f32[296,8192]{1,0:T(8,128)} %leaf_ref.1, f32[8,296,296]{2,1,0:T(8,128)} %m_ref.1), custom_call_target="tpu_custom_call" | custom-call | flops 4306501632 | bytes 12503040 | tf_op jit(solution)/shard_map/upward/pallas_call | solution.py:107
  22.8 0.0 all-to-all-done
  22.8 0.5 broadcast.179
  23.3 0.7 reduce.9
  24.0 0.6 reshape.148.wanted_ref
  24.6 5.8 %choose.2 = f32[32,152,128]{2,1,0:T(8,128)} custom-call(s32[64]{0:T(128)} %reshape.148.wanted_ref, f32[8,296,128]{2,1,0:T(8,128)} %get-tuple-element.9.pool_ref), custom_call_target="tpu_custom_call" | custom-call | bytes 3702784 | tf_op jit(solution)/shard_map/choose/pallas_call | solution.py:223
  30.4 0.0 copy-start.2
  30.4 5.8 %all-to-all-start.1 = ((f32[32,152,128]{2,1,0:T(8,128)}), f32[32,152,128]{2,1,0:T(8,128)S(1)}, u32[]{:S(2)}, u32[]{:S(2)}) async-start(f32[32,152,128]{2,1,0:T(8,128)} %choose.2), calls=%async_computation.1 | async-start | bytes 4980736 | tf_op jit(solution)/shard_map/all_to_all | solution.py:465
  36.3 0.1 copy.24
  36.3 0.1 broadcast_in_dim.44
  36.4 0.0 copy-done.2
  36.4 0.1 add.78
  36.5 0.2 select_reduce_fusion
  36.8 0.1 convert_reduce_fusion.3
  37.0 0.2 convert_reduce_fusion
  37.2 0.7 select_reduce_fusion.1.list_ref
  37.9 6.2 %coarse.1 = f32[296,64]{1,0:T(8,128)} custom-call(s32[1]{0:T(128)} %bitcast.first_ref, f32[8,296,128]{2,1,0:T(8,128)} %get-tuple-element.9.pool_ref, bf16[296,3072]{1,0:T(8,128)(2,1)} %get-tuple-element.11.mh_ref, bf16[296,3072]{1,0:T(8,128)(2,1)} %get-tuple-element.12.ml_ref), custom_call_target="tpu_custom_call" | custom-call | flops 1076625408 | bytes 4849664 | tf_op jit(solution)/shard_map/coarse/pallas_call | solution.py:164
  44.1 0.0 copy-start.1
  44.1 0.3 collective-permute-start
  44.3 0.7 slice_reduce_fusion
  45.1 5.8 %choose.3 = f32[32,152,128]{2,1,0:T(8,128)} custom-call(s32[64]{0:T(128)} %reshape.148.wanted_ref, f32[8,296,128]{2,1,0:T(8,128)} %get-tuple-element.9.pool_ref), custom_call_target="tpu_custom_call" | custom-call | bytes 3702784 | tf_op jit(solution)/shard_map/choose/pallas_call | solution.py:223
  50.9 0.0 collective-permute-done
  50.9 0.0 copy-done.1
  50.9 1.7 collective-permute-start.1
  52.6 22.9 %field.3.rest_0_ = f32[17,296,128]{2,1,0:T(8,128)} custom-call(f32[948]{0:T(1024)} %constant.75.clone.tbl_ref, s32[352]{0:T(512)} %select_reduce_fusion.1.list_ref, s32[2]{0:T(128)} %get-tuple-element.14.span_ref, f32[3,304,128]{2,1,0:T(8,128)} %constant.76.clone.col_ref, f32[8,384]{1,0:T(8,128)} %constant.77.clone.row_ref, ...), custom_call_target="tpu_custom_call" | custom-call | flops 6992953344 | bytes 1212416 | tf_op jit(solution)/shard_map/field/pallas_call | solution.py:416
  75.6 0.0 collective-permute-done.1
  75.6 0.1 dynamic-slice_add_fusion
  75.7 17.7 %all-to-all-done.1.pool_ref = f32[32,152,128]{2,1,0:T(8,128)S(1)} async-done(((f32[32,152,128]{2,1,0:T(8,128)}), f32[32,152,128]{2,1,0:T(8,128)S(1)}, u32[]{:S(2)}, u32[]{:S(2)}) %all-to-all-start.1) | async-done | bytes 2490400 | tf_op jit(solution)/shard_map/all_to_all | solution.py:465
  93.5 0.0 copy-start
  93.5 1.4 copy-done
  94.9 4.2 %all-to-all-start.2 = ((f32[32,152,128]{2,1,0:T(8,128)}), f32[32,152,128]{2,1,0:T(8,128)}, u32[]{:S(2)}, u32[]{:S(2)}) async-start(f32[32,152,128]{2,1,0:T(8,128)} %choose.3), calls=%async_computation.2 | async-start | bytes 4980736 | tf_op jit(solution)/shard_map/all_to_all | solution.py:465
  99.1 0.7 copy.25
  99.8 34.2 %field.4.rest_0_ = f32[17,296,128]{2,1,0:T(8,128)} custom-call(f32[948]{0:T(1024)} %constant.75.clone.tbl_ref, s32[352]{0:T(512)} %select_reduce_fusion.1.list_ref, s32[2]{0:T(128)} %get-tuple-element.26.span_ref, f32[3,304,128]{2,1,0:T(8,128)} %constant.76.clone.col_ref, f32[8,384]{1,0:T(8,128)} %constant.77.clone.row_ref, f32[32,152,128]{2,1,0:T(8,128)} %copy-done, ...), custom_call_target="tpu_custom_call" | custom-call | flops 6992953344 | bytes 2490368 | tf_op jit(solution)/shard_map/field/pallas_call | solution.py:416
  134.1 22.3 %all-to-all-done.2.pool_ref = f32[32,152,128]{2,1,0:T(8,128)} async-done(((f32[32,152,128]{2,1,0:T(8,128)}), f32[32,152,128]{2,1,0:T(8,128)}, u32[]{:S(2)}, u32[]{:S(2)}) %all-to-all-start.2) | async-done | bytes 2490400 | tf_op jit(solution)/shard_map/all_to_all | solution.py:465
  156.3 23.2 %field.5 = f32[296,1024]{1,0:T(8,128)} custom-call(f32[948]{0:T(1024)} %constant.75.clone.tbl_ref, s32[352]{0:T(512)} %select_reduce_fusion.1.list_ref, s32[2]{0:T(128)} %get-tuple-element.28.span_ref, f32[3,304,128]{2,1,0:T(8,128)} %constant.76.clone.col_ref, f32[8,384]{1,0:T(8,128)} %constant.77.clone.row_ref, f32[32,152,128]{2,1,0:T(8,128)} %all-to-all-done.2.pool_ref, ...), custom_call_target="tpu_custom_call" | custom-call | flops 6992953344 | bytes 2490368 | tf_op jit(solution)/shard_map/field/pallas_call | solution.py:416
  (6 shorter events, 0.1 us)
Async XLA Ops:
  2.6 20.1 %all-to-all-start = ((s32[32,1,2]{2,1,0:T(1,128)}), s32[32,1,2]{2,1,0:T(1,128)S(1)}, u32[]{:S(2)}, u32[]{:S(2)}) async-start(s32[32,1,2]{2,1,0:T(1,128)} %copy.23), calls=%async_computation | async-start | bytes 32768 | tf_op jit(solution)/shard_map/all_to_all | solution.py:465
  30.4 6.0 %copy-start.2 = (s32[16,22]{1,0:T(8,128)S(1)}, s32[16,22]{1,0:T(8,128)}, u32[]{:S(2)}) copy-start(s32[16,22]{1,0:T(8,128)} %param.16) | copy-start | bytes 4228
  30.4 63.0 %all-to-all-start.1 = ((f32[32,152,128]{2,1,0:T(8,128)}), f32[32,152,128]{2,1,0:T(8,128)S(1)}, u32[]{:S(2)}, u32[]{:S(2)}) async-start(f32[32,152,128]{2,1,0:T(8,128)} %choose.2), calls=%async_computation.1 | async-start | bytes 4980736 | tf_op jit(solution)/shard_map/all_to_all | solution.py:465
  44.1 6.8 %copy-start.1 = (f32[296,64]{1,0:T(8,128)S(1)}, f32[296,64]{1,0:T(8,128)}, u32[]{:S(2)}) copy-start(f32[296,64]{1,0:T(8,128)} %coarse.1) | copy-start | bytes 227332
  44.1 6.8 %collective-permute-start = (f32[296,64]{1,0:T(8,128)}, f32[296,64]{1,0:T(8,128)S(1)}, u32[]{:S(2)}, u32[]{:S(2)}) collective-permute-start(f32[296,64]{1,0:T(8,128)} %coarse.1), channel_id=1, source_target_pairs={{0,1},{1,0},{2,3},{3,2},{4,5},{5,4},{6,7},{7,6},{8,9},{9,8},{10,11... | collective-permute-start | bytes 227336 | tf_op jit(solution)/shard_map/ppermute | solution.py:484
  50.9 24.6 %collective-permute-start.1 = (f32[296,64]{1,0:T(8,128)S(1)}, f32[296,64]{1,0:T(8,128)S(1)}, u32[]{:S(2)}, u32[]{:S(2)}) collective-permute-start(f32[296,64]{1,0:T(8,128)S(1)} %add.72), channel_id=1, source_target_pairs={{0,2},{1,3},{2,0},{3,1},{4,6},{5,7},{6,4},{7,5},{8,10},{9,11},{10,... | collective-permute-start | bytes 227336 | tf_op jit(solution)/shard_map/ppermute | solution.py:484
  93.5 1.4 copy-start
  94.9 61.4 %all-to-all-start.2 = ((f32[32,152,128]{2,1,0:T(8,128)}), f32[32,152,128]{2,1,0:T(8,128)}, u32[]{:S(2)}, u32[]{:S(2)}) async-start(f32[32,152,128]{2,1,0:T(8,128)} %choose.3), calls=%async_computation.2 | async-start | bytes 4980736 | tf_op jit(solution)/shard_map/all_to_all | solution.py:465

commit v2 on v1

--- a/solution.py
+++ b/solution.py
@@ -193,23 +193,25 @@
     def send(dest):
         return pltpu.make_async_copy(ready.at[dest], out_ref.at[dest], sems.at[dest])
 
-    @pl.loop(0, count)
+    @pl.loop(0, count, unroll=4)
     def _(dest):
-        box = wanted_ref[CAP * dest + slot]
+        box = wanted_ref[dest, slot]
         slab = lax.shift_right_logical(box, 1)
         odd = (box & 1) == 1
         for start, rows in row_tiles(lower):
             under = pool_ref[slab, upper + start : upper + start + rows, :]
-            under = jnp.where(odd, under, half_turn(under))
             have = min(rows, upper - start)
             if have <= 0:
                 over = jnp.zeros_like(under)
             else:
                 over = pool_ref[slab, start : start + have, :]
-                over = jnp.where(odd, half_turn(over), over)
                 if have < rows:
                     over = jnp.concatenate([over, jnp.zeros((rows - have, LANES), f32)], axis=0)
-            ready[dest, start : start + rows, :] = jnp.where(low_lanes(rows), over, under)
+            turned = half_turn(jnp.where(odd, over, under))
+            low = low_lanes(rows)
+            ready[dest, start : start + rows, :] = jnp.where(
+                odd, jnp.where(low, turned, under), jnp.where(low, over, turned)
+            )
         send(dest).start()
 
     for dest in range(count):
@@ -230,7 +232,7 @@
             flops=0, bytes_accessed=4 * (pool.size + math.prod(shape)), transcendentals=0
         ),
         name="choose",
-    )(tie(wanted.reshape(-1), after), pool)
+    )(tie(wanted, after), pool)
 
 
 def tie(value, after):
@@ -241,21 +243,25 @@
 TAIL = 64
 
 
-def field_kernel(first, last, boxes, size, tbl_ref, list_ref, span_ref, col_ref, row_ref, pool_ref, *rest):
+def field_kernel(first, last, boxes, size, tbl_ref, list_ref, span_ref, col_ref, row_ref, pool_hbm, *rest):
     rest = list(rest)
-    acc_in = None if first else rest.pop(0)
-    out_ref, sp, dist = rest[:3]
-    rest = rest[3:]
-    acc = rest.pop(0) if last else out_ref
+    acc_hbm = None if first else rest.pop(0)
+    out_ref, acc, pool_ref, sp, dist, arrived, carried = rest
     slabs, held, _ = pool_ref.shape
     upper, lower = fold_rows(size)
     folded = held != size
     rows_pad = dist.shape[0]
+
+    def fetch(slab):
+        return pltpu.make_async_copy(pool_hbm.at[slab], pool_ref.at[slab], arrived.at[slab])
+
+    for slab in range(slabs):
+        fetch(slab).start()
     if first:
         acc[...] = jnp.zeros_like(acc)
     else:
-        carried = pltpu.make_async_copy(acc_in, acc, rest.pop(0))
-        carried.start()
+        acc_copy = pltpu.make_async_copy(acc_hbm, acc, carried)
+        acc_copy.start()
 
     for start, rows in row_tiles(rows_pad):
         for lane in range(0, KPAD, LANES):
@@ -269,6 +275,8 @@
 
     @pl.loop(0, slabs)
     def _(slab):
+        fetch(slab).wait()
+
         def keep(source, at, value):
             lesser = value - value.astype(bf16).astype(f32)
             sp[source, at : at + value.shape[0], :] = jnp.where(
@@ -298,7 +306,7 @@
             empty(source, ending)
 
     if not first:
-        carried.wait()
+        acc_copy.wait()
     begin = span_ref[0]
     count = span_ref[1]
 
@@ -376,7 +384,11 @@
     kinds = [pltpu.ACC(at % 2)((rows, 256), f32) for at, (_, rows) in tiles_of]
     pl.run_scoped(duos, *kinds, *kinds)
 
-    if last:
+    if not last:
+        result = pltpu.make_async_copy(acc, out_ref, carried)
+        result.start()
+        result.wait()
+    else:
         for slab in range(boxes // 2):
             for start, rows in row_tiles(size):
                 left = acc[2 * slab, start : start + rows, :]
@@ -400,23 +412,25 @@
     smem = pl.BlockSpec(memory_space=pltpu.SMEM)
     first = acc is None
     args = [jnp.asarray(offset_table().reshape(-1), f32), listing, tie(span, after), jnp.asarray(col), jnp.asarray(row), pool]
-    specs = [smem, smem, smem, vmem, vmem, vmem]
+    hbm = pl.BlockSpec(memory_space=pltpu.HBM)
+    specs = [smem, smem, smem, vmem, vmem, hbm]
     sums = (boxes + 1, size, LANES)
     scratch = [
+        pltpu.VMEM(sums, f32),
+        pltpu.VMEM(pool.shape, f32),
         pltpu.VMEM((sources, MAIN + TAIL, LANES), bf16),
         pltpu.VMEM((rows_pad, KPAD), f32),
+        pltpu.SemaphoreType.DMA((slabs,)),
+        pltpu.SemaphoreType.DMA,
     ]
-    if last:
-        scratch.append(pltpu.VMEM(sums, f32))
     if not first:
         args.append(acc)
-        specs.append(pl.BlockSpec(memory_space=pl.ANY))
-        scratch.append(pltpu.SemaphoreType.DMA)
+        specs.append(hbm)
     pairs = listing.shape[0] // 3
     return pl.pallas_call(
         functools.partial(field_kernel, first, last, boxes, size),
         in_specs=specs,
-        out_specs=vmem,
+        out_specs=vmem if last else hbm,
         out_shape=jax.ShapeDtypeStruct((size, boxes * LANES // 2) if last else sums, f32),
         scratch_shapes=scratch,
         compiler_params=pltpu.CompilerParams(vmem_limit_bytes=60 * 1024 * 1024),
@@ -457,7 +471,7 @@
     local = jnp.arange(box_count, dtype=jnp.int32)
     earlier = (local[None, :] < local[:, None])[None]
     rank = jnp.sum((needed[:, None, :] & earlier).astype(jnp.int32), axis=2)
-    slots = jnp.arange(CAP, dtype=jnp.int32)
+    slots = jnp.arange(LANES, dtype=jnp.int32)
     hit = needed[:, None, :] & (rank[:, None, :] == slots[None, :, None])
     wanted = jnp.sum(jnp.where(hit, local[None, None, :], 0), axis=2)
 
@@ -487,7 +501,7 @@
 
     chosen_second = choose(pool, requested, 1, chosen)
     acc = field(pool, None, listing, spans[0], box_count, size, False, chosen_second)
-    received_second = exchange(tie(chosen_second, (received, acc, coarse)))
+    received_second = exchange(tie(chosen_second, (acc, coarse)))
     acc = field(received, acc, listing, spans[1], box_count, size, False, None)
     out = field(received_second, acc, listing, spans[2], box_count, size, True, None)
     return (coarse, out)

time: 180 us -> 178 us (0.989)
  the two profiles are of different devices: /device:TPU:0 before, /device:TPU:26 now
where the time goes in v2:
time: 178 us; the launch traced here: 179 us
  Pallas kernels  109 us (61%)
  waiting for transfers between devices  42.7 us (24%)
  starting transfers between devices  18.8 us (11%)
  local copies, waits for them, and re-layouts  4.74 us (3%)
  other arithmetic  2.69 us (2%)
    pallas_call x3, Pallas kernels, field(): pl.pallas_call(functools.partial(field_kernel, first, last, boxes, size),...  83.1 us
    all_to_all x3, waiting for transfers between devices, exchange(): return lax.all_to_all(value, axes, split_axis=0, concat_axis=0, tiled=True)  42.7 us
    all_to_all x3, starting transfers between devices, exchange(): return lax.all_to_all(value, axes, split_axis=0, concat_axis=0, tiled=True)  18.1 us
    pallas_call x1, Pallas kernels, upward(): pl.pallas_call(upward_kernel, grid=(slabs // step,), in_specs=[pl.BlockSp...  12.8 us
    pallas_call x2, Pallas kernels, choose(): pl.pallas_call(functools.partial(choose_kernel, dests, slot), in_specs=[p...  6.88 us
    pallas_call x1, Pallas kernels, coarse_partial(): pl.pallas_call(coarse_kernel, in_specs=[pl.BlockSpec(memory_space=pltpu.S...  6.17 us
  transfers between devices with their start and end apart: 5, of which 2 were waited for; matrix products, arithmetic and copies ran while one was open for 2% of the time, Pallas kernels for 43%

profile of v2, /device:TPU:26, one launch (start us, length us, event | category | flops | bytes accessed | tf_op | source)
XLA Modules:
  0.0 178.6 jit_solution(12537993713371023985)
XLA Ops:
  0.6 0.8 eq.79
  1.4 0.2 fusion
  1.6 0.1 and.77
  1.7 0.1 copy.18
  1.8 0.1 convert_reduce_fusion.1
  1.9 0.1 copy.19
  2.0 0.8 select_reduce_fusion.2
  2.8 5.9 %all-to-all-start = ((s32[32,1,128]{2,1,0:T(1,128)}), s32[32,1,128]{2,1,0:T(1,128)S(1)}, u32[]{:S(2)}, u32[]{:S(2)}) async-start(s32[32,1,128]{2,1,0:T(1,128)} %bitcast.2), calls=%async_computation | async-start | bytes 32768 | tf_op jit(solution)/shard_map/all_to_all | solution.py:479
  8.7 12.8 %upward.1 = (f32[8,296,128]{2,1,0:T(8,128)}, bf16[296,3072]{1,0:T(8,128)(2,1)}, bf16[296,3072]{1,0:T(8,128)(2,1)}) custom-call(f32[296,8192]{1,0:T(8,128)} %leaf_ref.1, f32[8,296,296]{2,1,0:T(8,128)} %m_ref.1), custom_call_target="tpu_custom_call" | custom-call | flops 4306501632 | bytes 12503040 | tf_op jit(solution)/shard_map/upward/pallas_call | solution.py:107
  21.5 0.0 all-to-all-done
  21.5 0.0 copy-start.2
  21.5 0.6 copy-done.2
  22.1 3.4 %choose.2 = f32[32,152,128]{2,1,0:T(8,128)} custom-call(s32[32,128]{1,0:T(8,128)} %bitcast.7, f32[8,296,128]{2,1,0:T(8,128)} %get-tuple-element.9.pool_ref.pool_hbm), custom_call_target="tpu_custom_call" | custom-call | bytes 3702784 | tf_op jit(solution)/shard_map/choose/pallas_call | solution.py:225
  25.5 0.0 copy-start.3
  25.5 5.8 %all-to-all-start.2 = ((f32[32,152,128]{2,1,0:T(8,128)}), f32[32,152,128]{2,1,0:T(8,128)S(1)}, u32[]{:S(2)}, u32[]{:S(2)}) async-start(f32[32,152,128]{2,1,0:T(8,128)} %choose.2), calls=%async_computation.2 | async-start | bytes 4980736 | tf_op jit(solution)/shard_map/all_to_all | solution.py:479
  31.4 0.1 broadcast_in_dim.44
  31.5 0.0 copy-done.3
  31.5 0.1 add.78
  31.6 0.2 select_reduce_fusion
  31.9 0.1 convert_reduce_fusion.3
  32.0 0.2 convert_reduce_fusion
  32.3 0.7 select_reduce_fusion.1.list_ref
  33.0 6.2 %coarse.1 = f32[296,64]{1,0:T(8,128)} custom-call(s32[1]{0:T(128)} %bitcast.first_ref, f32[8,296,128]{2,1,0:T(8,128)} %get-tuple-element.9.pool_ref.pool_hbm, bf16[296,3072]{1,0:T(8,128)(2,1)} %get-tuple-element.11.mh_ref, bf16[296,3072]{1,0:T(8,128)(2,1)} %get-tuple-element.12.ml_ref), custom_call_target="tpu_custom_call" | custom-call | flops 1076625408 | bytes 4849664 | tf_op jit(solution)/shard_map/coarse/pallas_call | solution.py:164
  39.2 0.0 copy-start.1
  39.2 0.1 collective-permute-start
  39.3 0.8 slice_reduce_fusion
  40.1 3.4 %choose.3 = f32[32,152,128]{2,1,0:T(8,128)} custom-call(s32[32,128]{1,0:T(8,128)} %bitcast.8, f32[8,296,128]{2,1,0:T(8,128)} %get-tuple-element.9.pool_ref.pool_hbm), custom_call_target="tpu_custom_call" | custom-call | bytes 3702784 | tf_op jit(solution)/shard_map/choose/pallas_call | solution.py:225
  43.5 0.0 collective-permute-done
  43.5 0.0 copy-done.1
  43.6 0.6 collective-permute-start.1
  44.2 24.6 %field.3.rest_0_ = f32[17,296,128]{2,1,0:T(8,128)} custom-call(f32[948]{0:T(1024)} %constant.75.clone.tbl_ref, s32[352]{0:T(512)} %select_reduce_fusion.1.list_ref, s32[2]{0:T(128)} %get-tuple-element.14.span_ref, f32[3,304,128]{2,1,0:T(8,128)} %constant.76.clone.col_ref, f32[8,384]{1,0:T(8,128)} %constant.77.clone.row_ref, ...), custom_call_target="tpu_custom_call" | custom-call | flops 6992953344 | bytes 1212416 | tf_op jit(solution)/shard_map/field/pallas_call | solution.py:430
  68.8 0.0 collective-permute-done.1
  68.8 0.1 dynamic-slice_add_fusion
  68.9 17.5 %all-to-all-done.2.pool_hbm = f32[32,152,128]{2,1,0:T(8,128)S(1)} async-done(((f32[32,152,128]{2,1,0:T(8,128)}), f32[32,152,128]{2,1,0:T(8,128)S(1)}, u32[]{:S(2)}, u32[]{:S(2)}) %all-to-all-start.2) | async-done | bytes 2490400 | tf_op jit(solution)/shard_map/all_to_all | solution.py:479
  86.4 0.0 copy-start
  86.4 1.4 copy-done
  87.8 6.4 %all-to-all-start.1 = ((f32[32,152,128]{2,1,0:T(8,128)}), f32[32,152,128]{2,1,0:T(8,128)}, u32[]{:S(2)}, u32[]{:S(2)}) async-start(f32[32,152,128]{2,1,0:T(8,128)} %choose.3), calls=%async_computation.1 | async-start | bytes 4980736 | tf_op jit(solution)/shard_map/all_to_all | solution.py:479
  94.2 0.7 copy.22
  94.9 29.2 %field.4.rest_0_ = f32[17,296,128]{2,1,0:T(8,128)} custom-call(f32[948]{0:T(1024)} %constant.75.clone.tbl_ref, s32[352]{0:T(512)} %select_reduce_fusion.1.list_ref, s32[2]{0:T(128)} %get-tuple-element.26.span_ref, f32[3,304,128]{2,1,0:T(8,128)} %constant.76.clone.col_ref, f32[8,384]{1,0:T(8,128)} %constant.77.clone.row_ref, f32[32,152,128]{2,1,0:T(8,128)} %copy-done, ...), custom_call_target="tpu_custom_call" | custom-call | flops 6992953344 | bytes 2490368 | tf_op jit(solution)/shard_map/field/pallas_call | solution.py:430
  124.1 25.2 %all-to-all-done.1.pool_hbm = f32[32,152,128]{2,1,0:T(8,128)} async-done(((f32[32,152,128]{2,1,0:T(8,128)}), f32[32,152,128]{2,1,0:T(8,128)}, u32[]{:S(2)}, u32[]{:S(2)}) %all-to-all-start.1) | async-done | bytes 2490400 | tf_op jit(solution)/shard_map/all_to_all | solution.py:479
  149.3 29.3 %field.5 = f32[296,1024]{1,0:T(8,128)} custom-call(f32[948]{0:T(1024)} %constant.75.clone.tbl_ref, s32[352]{0:T(512)} %select_reduce_fusion.1.list_ref, s32[2]{0:T(128)} %get-tuple-element.28.span_ref, f32[3,304,128]{2,1,0:T(8,128)} %constant.76.clone.col_ref, f32[8,384]{1,0:T(8,128)} %constant.77.clone.row_ref, f32[32,152,128]{2,1,0:T(8,128)} %all-to-all-done.1.pool_hbm, ...), custom_call_target="tpu_custom_call" | custom-call | flops 6992953344 | bytes 2490368 | tf_op jit(solution)/shard_map/field/pallas_call | solution.py:430
  (5 shorter events, 0.1 us)
Async XLA Ops:
  2.8 18.7 %all-to-all-start = ((s32[32,1,128]{2,1,0:T(1,128)}), s32[32,1,128]{2,1,0:T(1,128)S(1)}, u32[]{:S(2)}, u32[]{:S(2)}) async-start(s32[32,1,128]{2,1,0:T(1,128)} %bitcast.2), calls=%async_computation | async-start | bytes 32768 | tf_op jit(solution)/shard_map/all_to_all | solution.py:479
  21.5 0.6 copy-start.2
  25.5 6.0 %copy-start.3 = (s32[16,22]{1,0:T(8,128)S(1)}, s32[16,22]{1,0:T(8,128)}, u32[]{:S(2)}) copy-start(s32[16,22]{1,0:T(8,128)} %param.16) | copy-start | bytes 4228
  25.5 60.9 %all-to-all-start.2 = ((f32[32,152,128]{2,1,0:T(8,128)}), f32[32,152,128]{2,1,0:T(8,128)S(1)}, u32[]{:S(2)}, u32[]{:S(2)}) async-start(f32[32,152,128]{2,1,0:T(8,128)} %choose.2), calls=%async_computation.2 | async-start | bytes 4980736 | tf_op jit(solution)/shard_map/all_to_all | solution.py:479
  39.2 4.4 %copy-start.1 = (f32[296,64]{1,0:T(8,128)S(1)}, f32[296,64]{1,0:T(8,128)}, u32[]{:S(2)}) copy-start(f32[296,64]{1,0:T(8,128)} %coarse.1) | copy-start | bytes 227332
  39.2 4.4 %collective-permute-start = (f32[296,64]{1,0:T(8,128)}, f32[296,64]{1,0:T(8,128)S(1)}, u32[]{:S(2)}, u32[]{:S(2)}) collective-permute-start(f32[296,64]{1,0:T(8,128)} %coarse.1), channel_id=1, source_target_pairs={{0,1},{1,0},{2,3},{3,2},{4,5},{5,4},{6,7},{7,6},{8,9},{9,8},{10,11... | collective-permute-start | bytes 227336 | tf_op jit(solution)/shard_map/ppermute | solution.py:498
  43.6 25.2 %collective-permute-start.1 = (f32[296,64]{1,0:T(8,128)S(1)}, f32[296,64]{1,0:T(8,128)S(1)}, u32[]{:S(2)}, u32[]{:S(2)}) collective-permute-start(f32[296,64]{1,0:T(8,128)S(1)} %add.72), channel_id=1, source_target_pairs={{0,2},{1,3},{2,0},{3,1},{4,6},{5,7},{6,4},{7,5},{8,10},{9,11},{10,... | collective-permute-start | bytes 227336 | tf_op jit(solution)/shard_map/ppermute | solution.py:498
  86.4 1.4 copy-start
  87.8 61.4 %all-to-all-start.1 = ((f32[32,152,128]{2,1,0:T(8,128)}), f32[32,152,128]{2,1,0:T(8,128)}, u32[]{:S(2)}, u32[]{:S(2)}) async-start(f32[32,152,128]{2,1,0:T(8,128)} %choose.3), calls=%async_computation.1 | async-start | bytes 4980736 | tf_op jit(solution)/shard_map/all_to_all | solution.py:479

commit v3 on v2

--- a/solution.py
+++ b/solution.py
@@ -243,10 +243,12 @@
 TAIL = 64
 
 
-def field_kernel(first, last, boxes, size, tbl_ref, list_ref, span_ref, col_ref, row_ref, pool_hbm, *rest):
+def field_kernel(
+    first, last, boxes, size, tbl_ref, list_ref, span_ref, there_ref, col_ref, row_ref, pool_hbm, *rest
+):
     rest = list(rest)
     acc_hbm = None if first else rest.pop(0)
-    out_ref, acc, pool_ref, sp, dist, arrived, carried = rest
+    out_ref, acc, pool_ref, sp, dist, arrived, carried, *done = rest
     slabs, held, _ = pool_ref.shape
     upper, lower = fold_rows(size)
     folded = held != size
@@ -256,7 +258,7 @@
         return pltpu.make_async_copy(pool_hbm.at[slab], pool_ref.at[slab], arrived.at[slab])
 
     for slab in range(slabs):
-        fetch(slab).start()
+        pl.when(there_ref[slab] > 0)(fetch(slab).start)
     if first:
         acc[...] = jnp.zeros_like(acc)
     else:
@@ -273,8 +275,7 @@
                 total = total + delta * delta
             dist[start : start + rows, lane : lane + LANES] = total
 
-    @pl.loop(0, slabs)
-    def _(slab):
+    def prepare(slab):
         fetch(slab).wait()
 
         def keep(source, at, value):
@@ -304,6 +305,10 @@
         ending = -(-size // 16) * 16
         for source in (slab,) if folded else (2 * slab, 2 * slab + 1):
             empty(source, ending)
+
+    @pl.loop(0, slabs)
+    def _(slab):
+        pl.when(there_ref[slab] > 0)(functools.partial(prepare, slab))
 
     if not first:
         acc_copy.wait()
@@ -389,16 +394,25 @@
         result.start()
         result.wait()
     else:
+        ready, sems = done
+
+        def send(slab):
+            lanes = pl.ds(slab * LANES, LANES)
+            return pltpu.make_async_copy(ready.at[:, lanes], out_ref.at[:, lanes], sems.at[slab])
+
         for slab in range(boxes // 2):
             for start, rows in row_tiles(size):
                 left = acc[2 * slab, start : start + rows, :]
                 right = acc[2 * slab + 1, start : start + rows, :]
-                out_ref[start : start + rows, slab * LANES : (slab + 1) * LANES] = kernel_scale * jnp.where(
+                ready[start : start + rows, slab * LANES : (slab + 1) * LANES] = kernel_scale * jnp.where(
                     low_lanes(rows), left + half_turn(left), right + half_turn(right)
                 )
-
-
-def field(pool, acc, listing, span, boxes, size, last, after):
+            send(slab).start()
+        for slab in range(boxes // 2):
+            send(slab).wait()
+
+
+def field(pool, acc, listing, span, there, boxes, size, last, after):
     slabs, held, _ = pool.shape
     sources = slabs if held != size else 2 * slabs
     points = surface_points(size) * radius
@@ -411,9 +425,9 @@
     vmem = pl.BlockSpec(memory_space=pltpu.VMEM)
     smem = pl.BlockSpec(memory_space=pltpu.SMEM)
     first = acc is None
-    args = [jnp.asarray(offset_table().reshape(-1), f32), listing, tie(span, after), jnp.asarray(col), jnp.asarray(row), pool]
+    args = [jnp.asarray(offset_table().reshape(-1), f32), listing, tie(span, after), there, jnp.asarray(col), jnp.asarray(row), pool]
     hbm = pl.BlockSpec(memory_space=pltpu.HBM)
-    specs = [smem, smem, smem, vmem, vmem, hbm]
+    specs = [smem, smem, smem, smem, vmem, vmem, hbm]
     sums = (boxes + 1, size, LANES)
     scratch = [
         pltpu.VMEM(sums, f32),
@@ -423,6 +437,11 @@
         pltpu.SemaphoreType.DMA((slabs,)),
         pltpu.SemaphoreType.DMA,
     ]
+    if last:
+        scratch += [
+            pltpu.VMEM((size, boxes * LANES // 2), f32),
+            pltpu.SemaphoreType.DMA((boxes // 2,)),
+        ]
     if not first:
         args.append(acc)
         specs.append(hbm)
@@ -430,10 +449,10 @@
     return pl.pallas_call(
         functools.partial(field_kernel, first, last, boxes, size),
         in_specs=specs,
-        out_specs=vmem if last else hbm,
+        out_specs=pl.BlockSpec(memory_space=pl.ANY) if last else hbm,
         out_shape=jax.ShapeDtypeStruct((size, boxes * LANES // 2) if last else sums, f32),
         scratch_shapes=scratch,
-        compiler_params=pltpu.CompilerParams(vmem_limit_bytes=60 * 1024 * 1024),
+        compiler_params=pltpu.CompilerParams(vmem_limit_bytes=67043328),
         cost_estimate=pl.CostEstimate(
             flops=2 * rows_pad * 2 * KPAD * LANES * pairs,
             bytes_accessed=4 * pool.size,
@@ -500,10 +519,12 @@
     coarse = lax.dynamic_slice_in_dim(current, (device % group_size) * share, share, 1)
 
     chosen_second = choose(pool, requested, 1, chosen)
-    acc = field(pool, None, listing, spans[0], box_count, size, False, chosen_second)
+    there = jnp.sum(needed.astype(jnp.int32), axis=1)
+    every = jnp.ones((box_count // 2,), jnp.int32)
+    acc = field(pool, None, listing, spans[0], every, box_count, size, False, chosen_second)
     received_second = exchange(tie(chosen_second, (acc, coarse)))
-    acc = field(received, acc, listing, spans[1], box_count, size, False, None)
-    out = field(received_second, acc, listing, spans[2], box_count, size, True, None)
+    acc = field(received, acc, listing, spans[1], there, box_count, size, False, None)
+    out = field(received_second, acc, listing, spans[2], there - 1, box_count, size, True, None)
     return (coarse, out)
 
 

time: 178 us -> 171 us (0.961)
  the two profiles are of different devices: /device:TPU:26 before, /device:TPU:4 now
where the time goes in v3:
time: 171 us; the launch traced here: 169 us
  Pallas kernels  106 us (62%)
  waiting for transfers between devices  35 us (20%)
  starting transfers between devices  18.1 us (11%)
  other arithmetic  5.01 us (3%)
  local copies, waits for them, and re-layouts  4.3 us (3%)
    pallas_call x3, Pallas kernels, field(): pl.pallas_call(functools.partial(field_kernel, first, last, boxes, size),...  79.7 us
    all_to_all x3, waiting for transfers between devices, exchange(): return lax.all_to_all(value, axes, split_axis=0, concat_axis=0, tiled=True)  35 us
    all_to_all x3, starting transfers between devices, exchange(): return lax.all_to_all(value, axes, split_axis=0, concat_axis=0, tiled=True)  16.5 us
    pallas_call x1, Pallas kernels, upward(): pl.pallas_call(upward_kernel, grid=(slabs // step,), in_specs=[pl.BlockSp...  12.8 us
    pallas_call x2, Pallas kernels, choose(): pl.pallas_call(functools.partial(choose_kernel, dests, slot), in_specs=[p...  6.92 us
    pallas_call x1, Pallas kernels, coarse_partial(): pl.pallas_call(coarse_kernel, in_specs=[pl.BlockSpec(memory_space=pltpu.S...  6.17 us
  transfers between devices with their start and end apart: 5, of which 2 were waited for; matrix products, arithmetic and copies ran while one was open for 4% of the time, Pallas kernels for 49%

profile of v3, /device:TPU:4, one launch (start us, length us, event | category | flops | bytes accessed | tf_op | source)
XLA Modules:
  0.0 168.9 jit_solution(9083030797349194388)
XLA Ops:
  0.6 0.8 eq.79
  1.4 0.2 fusion
  1.6 0.1 and.77
  1.7 0.0 copy-start.2
  1.7 0.1 copy.18
  1.8 0.1 convert_reduce_fusion.1
  1.9 0.1 copy.19
  2.0 0.8 select_reduce_fusion.2
  2.8 6.1 %all-to-all-start = ((s32[32,1,128]{2,1,0:T(1,128)}), s32[32,1,128]{2,1,0:T(1,128)S(1)}, u32[]{:S(2)}, u32[]{:S(2)}) async-start(s32[32,1,128]{2,1,0:T(1,128)} %bitcast.2), calls=%async_computation | async-start | bytes 32768 | tf_op jit(solution)/shard_map/all_to_all | solution.py:498
  8.9 12.8 %upward.1 = (f32[8,296,128]{2,1,0:T(8,128)}, bf16[296,3072]{1,0:T(8,128)(2,1)}, bf16[296,3072]{1,0:T(8,128)(2,1)}) custom-call(f32[296,8192]{1,0:T(8,128)} %leaf_ref.1, f32[8,296,296]{2,1,0:T(8,128)} %m_ref.1), custom_call_target="tpu_custom_call" | custom-call | flops 4306501632 | bytes 12503040 | tf_op jit(solution)/shard_map/upward/pallas_call | solution.py:107
  21.7 0.0 copy-done.2
  21.7 0.0 all-to-all-done
  21.7 0.0 copy-start.1
  21.7 0.6 copy-done.1
  22.3 3.5 %choose.2 = f32[32,152,128]{2,1,0:T(8,128)} custom-call(s32[32,128]{1,0:T(8,128)} %bitcast.7, f32[8,296,128]{2,1,0:T(8,128)} %get-tuple-element.9.pool_ref.pool_hbm), custom_call_target="tpu_custom_call" | custom-call | bytes 3702784 | tf_op jit(solution)/shard_map/choose/pallas_call | solution.py:225
  25.8 0.0 copy-start.4
  25.8 5.9 %all-to-all-start.2 = ((f32[32,152,128]{2,1,0:T(8,128)}), f32[32,152,128]{2,1,0:T(8,128)}, u32[]{:S(2)}, u32[]{:S(2)}) async-start(f32[32,152,128]{2,1,0:T(8,128)} %choose.2), calls=%async_computation.2 | async-start | bytes 4980736 | tf_op jit(solution)/shard_map/all_to_all | solution.py:498
  31.7 0.1 broadcast_in_dim.44
  31.8 0.0 copy-done.4
  31.8 0.1 add.79
  31.9 0.2 select_reduce_fusion
  32.2 0.1 convert_reduce_fusion.4
  32.3 0.2 convert_reduce_fusion
  32.6 0.7 select_reduce_fusion.1.list_ref
  33.3 6.2 %coarse.1 = f32[296,64]{1,0:T(8,128)} custom-call(s32[1]{0:T(128)} %bitcast.first_ref, f32[8,296,128]{2,1,0:T(8,128)} %get-tuple-element.9.pool_ref.pool_hbm, bf16[296,3072]{1,0:T(8,128)(2,1)} %get-tuple-element.11.mh_ref, bf16[296,3072]{1,0:T(8,128)(2,1)} %get-tuple-element.12.ml_ref), custom_call_target="tpu_custom_call" | custom-call | flops 1076625408 | bytes 4849664 | tf_op jit(solution)/shard_map/coarse/pallas_call | solution.py:164
  39.5 0.0 copy-start
  39.5 0.1 collective-permute-start
  39.6 0.8 slice_reduce_fusion
  40.3 3.5 %choose.3 = f32[32,152,128]{2,1,0:T(8,128)} custom-call(s32[32,128]{1,0:T(8,128)} %bitcast.8, f32[8,296,128]{2,1,0:T(8,128)} %get-tuple-element.9.pool_ref.pool_hbm), custom_call_target="tpu_custom_call" | custom-call | bytes 3702784 | tf_op jit(solution)/shard_map/choose/pallas_call | solution.py:225
  43.8 0.0 collective-permute-done
  43.8 0.0 copy-done
  43.8 0.7 add.73
  44.5 1.5 collective-permute-start.1
  46.0 0.5 broadcast_3_there_ref.2.there_ref
  46.5 28.6 %field.3.rest_0_ = f32[17,296,128]{2,1,0:T(8,128)} custom-call(f32[948]{0:T(1024)} %constant.78.clone.tbl_ref, s32[352]{0:T(512)} %select_reduce_fusion.1.list_ref, s32[2]{0:T(128)} %get-tuple-element.14.span_ref, s32[8]{0:T(128)} %broadcast_3_there_ref.2.there_ref, f32[3,304,128]{2,1,0:T(8,128)} %constant.79.clone.col_ref, ...), custom_call_target="tpu_custom_call" | custom-call | flops 6992953344 | bytes 1212416 | tf_op jit(solution)/shard_map/field/pallas_call | solution.py:449
  75.1 0.0 collective-permute-done.1
  75.1 1.1 dynamic-slice_add_fusion
  76.2 0.0 copy-start.3
  76.2 12.3 %all-to-all-done.2.pool_hbm = f32[32,152,128]{2,1,0:T(8,128)} async-done(((f32[32,152,128]{2,1,0:T(8,128)}), f32[32,152,128]{2,1,0:T(8,128)}, u32[]{:S(2)}, u32[]{:S(2)}) %all-to-all-start.2) | async-done | bytes 2490400 | tf_op jit(solution)/shard_map/all_to_all | solution.py:498
  88.6 4.5 %all-to-all-start.1 = ((f32[32,152,128]{2,1,0:T(8,128)}), f32[32,152,128]{2,1,0:T(8,128)}, u32[]{:S(2)}, u32[]{:S(2)}) async-start(f32[32,152,128]{2,1,0:T(8,128)} %choose.3), calls=%async_computation.1 | async-start | bytes 4980736 | tf_op jit(solution)/shard_map/all_to_all | solution.py:498
  93.1 0.0 copy-done.3
  93.2 0.1 convert_reduce_fusion.2.there_ref
  93.3 0.5 copy-done.5
  93.8 0.6 broadcast_add_fusion.there_ref
  94.4 0.7 copy.22
  95.1 32.3 %field.4.rest_0_ = f32[17,296,128]{2,1,0:T(8,128)} custom-call(f32[948]{0:T(1024)} %constant.78.clone.tbl_ref, s32[352]{0:T(512)} %select_reduce_fusion.1.list_ref, s32[2]{0:T(128)} %get-tuple-element.26.span_ref, s32[32]{0:T(128)} %copy-done.5, f32[3,304,128]{2,1,0:T(8,128)} %constant.79.clone.col_ref, f32[8,384]{1,0:T(8,128)} %constant.80.clone.row_ref, ...), custom_call_target="tpu_custom_call" | custom-call | flops 6992953344 | bytes 2490368 | tf_op jit(solution)/shard_map/field/pallas_call | solution.py:449
  127.4 22.7 %all-to-all-done.1.pool_hbm = f32[32,152,128]{2,1,0:T(8,128)} async-done(((f32[32,152,128]{2,1,0:T(8,128)}), f32[32,152,128]{2,1,0:T(8,128)}, u32[]{:S(2)}, u32[]{:S(2)}) %all-to-all-start.1) | async-done | bytes 2490400 | tf_op jit(solution)/shard_map/all_to_all | solution.py:498
  150.0 18.8 %field.5 = f32[296,1024]{1,0:T(8,128)} custom-call(f32[948]{0:T(1024)} %constant.78.clone.tbl_ref, s32[352]{0:T(512)} %select_reduce_fusion.1.list_ref, s32[2]{0:T(128)} %get-tuple-element.28.span_ref, s32[32]{0:T(128)} %broadcast_add_fusion.there_ref, f32[3,304,128]{2,1,0:T(8,128)} %constant.79.clone.col_ref, f32[8,384]{1,0:T(8,128)} %constant.80.clone.row_ref, ...), custom_call_target="tpu_custom_call" | custom-call | flops 6992953344 | bytes 2490368 | tf_op jit(solution)/shard_map/field/pallas_call | solution.py:449
  (5 shorter events, 0.0 us)
Async XLA Ops:
  1.7 20.0 %copy-start.2 = (pred[32,16]{1,0:T(8,128)(4,1)}, pred[32,16]{1,0:T(8,128)(4,1)S(1)}, u32[]{:S(2)}) copy-start(pred[32,16]{1,0:T(8,128)(4,1)S(1)} %and.77) | copy-start | bytes 1540
  2.8 18.9 %all-to-all-start = ((s32[32,1,128]{2,1,0:T(1,128)}), s32[32,1,128]{2,1,0:T(1,128)S(1)}, u32[]{:S(2)}, u32[]{:S(2)}) async-start(s32[32,1,128]{2,1,0:T(1,128)} %bitcast.2), calls=%async_computation | async-start | bytes 32768 | tf_op jit(solution)/shard_map/all_to_all | solution.py:498
  21.7 0.6 copy-start.1
  25.8 6.0 %copy-start.4 = (s32[16,22]{1,0:T(8,128)S(1)}, s32[16,22]{1,0:T(8,128)}, u32[]{:S(2)}) copy-start(s32[16,22]{1,0:T(8,128)} %param.16) | copy-start | bytes 4228
  25.8 62.8 %all-to-all-start.2 = ((f32[32,152,128]{2,1,0:T(8,128)}), f32[32,152,128]{2,1,0:T(8,128)}, u32[]{:S(2)}, u32[]{:S(2)}) async-start(f32[32,152,128]{2,1,0:T(8,128)} %choose.2), calls=%async_computation.2 | async-start | bytes 4980736 | tf_op jit(solution)/shard_map/all_to_all | solution.py:498
  39.5 4.3 %copy-start = (f32[296,64]{1,0:T(8,128)S(1)}, f32[296,64]{1,0:T(8,128)}, u32[]{:S(2)}) copy-start(f32[296,64]{1,0:T(8,128)} %coarse.1) | copy-start | bytes 227332
  39.5 4.3 %collective-permute-start = (f32[296,64]{1,0:T(8,128)}, f32[296,64]{1,0:T(8,128)S(1)}, u32[]{:S(2)}, u32[]{:S(2)}) collective-permute-start(f32[296,64]{1,0:T(8,128)} %coarse.1), channel_id=1, source_target_pairs={{0,1},{1,0},{2,3},{3,2},{4,5},{5,4},{6,7},{7,6},{8,9},{9,8},{10,11... | collective-permute-start | bytes 227336 | tf_op jit(solution)/shard_map/ppermute | solution.py:517
  44.5 30.6 %collective-permute-start.1 = (f32[296,64]{1,0:T(8,128)}, f32[296,64]{1,0:T(8,128)}, u32[]{:S(2)}, u32[]{:S(2)}) collective-permute-start(f32[296,64]{1,0:T(8,128)} %add.73), channel_id=1, source_target_pairs={{0,2},{1,3},{2,0},{3,1},{4,6},{5,7},{6,4},{7,5},{8,10},{9,11},{10,... | collective-permute-start | bytes 227336 | tf_op jit(solution)/shard_map/ppermute | solution.py:517
  76.2 16.9 %copy-start.3 = (pred[32,16]{1,0:T(8,128)(4,1)S(1)}, pred[32,16]{1,0:T(8,128)(4,1)}, u32[]{:S(2)}) copy-start(pred[32,16]{1,0:T(8,128)(4,1)} %copy-done.2) | copy-start | bytes 1540
  88.6 61.4 %all-to-all-start.1 = ((f32[32,152,128]{2,1,0:T(8,128)}), f32[32,152,128]{2,1,0:T(8,128)}, u32[]{:S(2)}, u32[]{:S(2)}) async-start(f32[32,152,128]{2,1,0:T(8,128)} %choose.3), calls=%async_computation.1 | async-start | bytes 4980736 | tf_op jit(solution)/shard_map/all_to_all | solution.py:498
  93.3 0.5 copy-start.5

commit v4 on v3

--- a/solution.py
+++ b/solution.py
@@ -74,11 +74,14 @@
 
     @pl.when(pl.program_id(0) == 0)
     def _():
-        mh_ref[...] = jnp.zeros_like(mh_ref)
-        ml_ref[...] = jnp.zeros_like(ml_ref)
-        xh[...] = jnp.zeros_like(xh)
-        xl[...] = jnp.zeros_like(xl)
+        lane, line = size // LANES * LANES, size // 16 * 16
         for child in range(8):
+            for ref in (mh_ref, ml_ref):
+                ref[:, child * KPAD + lane : (child + 1) * KPAD] = jnp.zeros((size, KPAD - lane), bf16)
+            for ref in (xh, xl):
+                ref[child * KPAD + line : (child + 1) * KPAD, :] = jnp.zeros(
+                    (KPAD - line, ref.shape[1]), bf16
+                )
             for start, rows in row_tiles(size):
                 split_store(
                     m_ref[child, start : start + rows, :], rows, mh_ref, ml_ref, start, child * KPAD, size
@@ -193,7 +196,7 @@
     def send(dest):
         return pltpu.make_async_copy(ready.at[dest], out_ref.at[dest], sems.at[dest])
 
-    @pl.loop(0, count, unroll=4)
+    @pl.loop(0, count, unroll=8)
     def _(dest):
         box = wanted_ref[dest, slot]
         slab = lax.shift_right_logical(box, 1)

time: 171 us -> 174 us (1.018)
  the two profiles are of different devices: /device:TPU:4 before, /device:TPU:0 now
where the time goes in v4:
time: 174 us
  Pallas kernels  105 us (60%)
  waiting for transfers between devices  39.7 us (23%)
  starting transfers between devices  19.2 us (11%)
  other arithmetic  5.01 us (3%)
  local copies, waits for them, and re-layouts  4.3 us (2%)
    pallas_call x3, Pallas kernels, field(): pl.pallas_call(functools.partial(field_kernel, first, last, boxes, size),...  79.9 us
    all_to_all x3, waiting for transfers between devices, exchange(): return lax.all_to_all(value, axes, split_axis=0, concat_axis=0, tiled=True)  39.7 us
    all_to_all x3, starting transfers between devices, exchange(): return lax.all_to_all(value, axes, split_axis=0, concat_axis=0, tiled=True)  17.4 us
    pallas_call x1, Pallas kernels, upward(): pl.pallas_call(upward_kernel, grid=(slabs // step,), in_specs=[pl.BlockSp...  12.8 us
    pallas_call x2, Pallas kernels, choose(): pl.pallas_call(functools.partial(choose_kernel, dests, slot), in_specs=[p...  6.45 us
    pallas_call x1, Pallas kernels, coarse_partial(): pl.pallas_call(coarse_kernel, in_specs=[pl.BlockSpec(memory_space=pltpu.S...  6.17 us
  transfers between devices with their start and end apart: 5, of which 2 were waited for; matrix products, arithmetic and copies ran while one was open for 3% of the time, Pallas kernels for 45%

profile of v4, /device:TPU:0, one launch (start us, length us, event | category | flops | bytes accessed | tf_op | source)
XLA Modules:
  0.0 174.4 jit_solution(2778025691908536231)
XLA Ops:
  0.6 0.8 eq.79
  1.4 0.2 fusion
  1.6 0.1 and.77
  1.7 0.0 copy-start.2
  1.7 0.1 copy.18
  1.8 0.1 convert_reduce_fusion.1
  1.9 0.1 copy.19
  2.0 0.8 select_reduce_fusion.2
  2.8 7.3 %all-to-all-start = ((s32[32,1,128]{2,1,0:T(1,128)}), s32[32,1,128]{2,1,0:T(1,128)S(1)}, u32[]{:S(2)}, u32[]{:S(2)}) async-start(s32[32,1,128]{2,1,0:T(1,128)} %bitcast.2), calls=%async_computation | async-start | bytes 32768 | tf_op jit(solution)/shard_map/all_to_all | solution.py:501
  10.2 12.8 %upward.1 = (f32[8,296,128]{2,1,0:T(8,128)}, bf16[296,3072]{1,0:T(8,128)(2,1)}, bf16[296,3072]{1,0:T(8,128)(2,1)}) custom-call(f32[296,8192]{1,0:T(8,128)} %leaf_ref.1, f32[8,296,296]{2,1,0:T(8,128)} %m_ref.1), custom_call_target="tpu_custom_call" | custom-call | flops 4306501632 | bytes 12503040 | tf_op jit(solution)/shard_map/upward/pallas_call | solution.py:110
  22.9 0.0 copy-done.2
  22.9 0.0 all-to-all-done
  23.0 0.0 copy-start.1
  23.0 0.6 copy-done.1
  23.6 3.2 %choose.2 = f32[32,152,128]{2,1,0:T(8,128)} custom-call(s32[32,128]{1,0:T(8,128)} %bitcast.7, f32[8,296,128]{2,1,0:T(8,128)} %get-tuple-element.9.pool_ref.pool_hbm), custom_call_target="tpu_custom_call" | custom-call | bytes 3702784 | tf_op jit(solution)/shard_map/choose/pallas_call | solution.py:228
  26.8 0.0 copy-start.4
  26.8 5.9 %all-to-all-start.2 = ((f32[32,152,128]{2,1,0:T(8,128)}), f32[32,152,128]{2,1,0:T(8,128)}, u32[]{:S(2)}, u32[]{:S(2)}) async-start(f32[32,152,128]{2,1,0:T(8,128)} %choose.2), calls=%async_computation.2 | async-start | bytes 4980736 | tf_op jit(solution)/shard_map/all_to_all | solution.py:501
  32.8 0.1 broadcast_in_dim.44
  32.9 0.0 copy-done.4
  32.9 0.1 add.79
  33.0 0.2 select_reduce_fusion
  33.2 0.1 convert_reduce_fusion.4
  33.4 0.2 convert_reduce_fusion
  33.6 0.7 select_reduce_fusion.1.list_ref
  34.3 6.2 %coarse.1 = f32[296,64]{1,0:T(8,128)} custom-call(s32[1]{0:T(128)} %bitcast.first_ref, f32[8,296,128]{2,1,0:T(8,128)} %get-tuple-element.9.pool_ref.pool_hbm, bf16[296,3072]{1,0:T(8,128)(2,1)} %get-tuple-element.11.mh_ref, bf16[296,3072]{1,0:T(8,128)(2,1)} %get-tuple-element.12.ml_ref), custom_call_target="tpu_custom_call" | custom-call | flops 1076625408 | bytes 4849664 | tf_op jit(solution)/shard_map/coarse/pallas_call | solution.py:167
  40.5 0.0 copy-start
  40.5 0.2 collective-permute-start
  40.7 0.8 slice_reduce_fusion
  41.5 3.2 %choose.3 = f32[32,152,128]{2,1,0:T(8,128)} custom-call(s32[32,128]{1,0:T(8,128)} %bitcast.8, f32[8,296,128]{2,1,0:T(8,128)} %get-tuple-element.9.pool_ref.pool_hbm), custom_call_target="tpu_custom_call" | custom-call | bytes 3702784 | tf_op jit(solution)/shard_map/choose/pallas_call | solution.py:228
  44.7 0.0 collective-permute-done
  44.7 0.0 copy-done
  44.7 0.7 add.73
  45.4 1.6 collective-permute-start.1
  47.0 0.5 broadcast_3_there_ref.2.there_ref
  47.5 29.1 %field.3.rest_0_ = f32[17,296,128]{2,1,0:T(8,128)} custom-call(f32[948]{0:T(1024)} %constant.78.clone.tbl_ref, s32[352]{0:T(512)} %select_reduce_fusion.1.list_ref, s32[2]{0:T(128)} %get-tuple-element.14.span_ref, s32[8]{0:T(128)} %broadcast_3_there_ref.2.there_ref, f32[3,304,128]{2,1,0:T(8,128)} %constant.79.clone.col_ref, ...), custom_call_target="tpu_custom_call" | custom-call | flops 6992953344 | bytes 1212416 | tf_op jit(solution)/shard_map/field/pallas_call | solution.py:452
  76.7 0.0 collective-permute-done.1
  76.7 1.1 dynamic-slice_add_fusion
  77.8 0.0 copy-start.3
  77.8 12.2 %all-to-all-done.2.pool_hbm = f32[32,152,128]{2,1,0:T(8,128)} async-done(((f32[32,152,128]{2,1,0:T(8,128)}), f32[32,152,128]{2,1,0:T(8,128)}, u32[]{:S(2)}, u32[]{:S(2)}) %all-to-all-start.2) | async-done | bytes 2490400 | tf_op jit(solution)/shard_map/all_to_all | solution.py:501
  90.0 4.2 %all-to-all-start.1 = ((f32[32,152,128]{2,1,0:T(8,128)}), f32[32,152,128]{2,1,0:T(8,128)}, u32[]{:S(2)}, u32[]{:S(2)}) async-start(f32[32,152,128]{2,1,0:T(8,128)} %choose.3), calls=%async_computation.1 | async-start | bytes 4980736 | tf_op jit(solution)/shard_map/all_to_all | solution.py:501
  94.2 0.0 copy-done.3
  94.2 0.1 convert_reduce_fusion.2.there_ref
  94.3 0.5 copy-done.5
  94.8 0.6 broadcast_add_fusion.there_ref
  95.4 0.7 copy.22
  96.1 27.7 %field.4.rest_0_ = f32[17,296,128]{2,1,0:T(8,128)} custom-call(f32[948]{0:T(1024)} %constant.78.clone.tbl_ref, s32[352]{0:T(512)} %select_reduce_fusion.1.list_ref, s32[2]{0:T(128)} %get-tuple-element.26.span_ref, s32[32]{0:T(128)} %copy-done.5, f32[3,304,128]{2,1,0:T(8,128)} %constant.79.clone.col_ref, f32[8,384]{1,0:T(8,128)} %constant.80.clone.row_ref, ...), custom_call_target="tpu_custom_call" | custom-call | flops 6992953344 | bytes 2490368 | tf_op jit(solution)/shard_map/field/pallas_call | solution.py:452
  123.9 27.5 %all-to-all-done.1.pool_hbm = f32[32,152,128]{2,1,0:T(8,128)} async-done(((f32[32,152,128]{2,1,0:T(8,128)}), f32[32,152,128]{2,1,0:T(8,128)}, u32[]{:S(2)}, u32[]{:S(2)}) %all-to-all-start.1) | async-done | bytes 2490400 | tf_op jit(solution)/shard_map/all_to_all | solution.py:501
  151.4 23.0 %field.5 = f32[296,1024]{1,0:T(8,128)} custom-call(f32[948]{0:T(1024)} %constant.78.clone.tbl_ref, s32[352]{0:T(512)} %select_reduce_fusion.1.list_ref, s32[2]{0:T(128)} %get-tuple-element.28.span_ref, s32[32]{0:T(128)} %broadcast_add_fusion.there_ref, f32[3,304,128]{2,1,0:T(8,128)} %constant.79.clone.col_ref, f32[8,384]{1,0:T(8,128)} %constant.80.clone.row_ref, ...), custom_call_target="tpu_custom_call" | custom-call | flops 6992953344 | bytes 2490368 | tf_op jit(solution)/shard_map/field/pallas_call | solution.py:452
  (5 shorter events, 0.0 us)
Async XLA Ops:
  1.7 21.2 %copy-start.2 = (pred[32,16]{1,0:T(8,128)(4,1)}, pred[32,16]{1,0:T(8,128)(4,1)S(1)}, u32[]{:S(2)}) copy-start(pred[32,16]{1,0:T(8,128)(4,1)S(1)} %and.77) | copy-start | bytes 1540
  2.8 20.1 %all-to-all-start = ((s32[32,1,128]{2,1,0:T(1,128)}), s32[32,1,128]{2,1,0:T(1,128)S(1)}, u32[]{:S(2)}, u32[]{:S(2)}) async-start(s32[32,1,128]{2,1,0:T(1,128)} %bitcast.2), calls=%async_computation | async-start | bytes 32768 | tf_op jit(solution)/shard_map/all_to_all | solution.py:501
  23.0 0.6 copy-start.1
  26.8 6.1 %copy-start.4 = (s32[16,22]{1,0:T(8,128)S(1)}, s32[16,22]{1,0:T(8,128)}, u32[]{:S(2)}) copy-start(s32[16,22]{1,0:T(8,128)} %param.16) | copy-start | bytes 4228
  26.8 63.2 %all-to-all-start.2 = ((f32[32,152,128]{2,1,0:T(8,128)}), f32[32,152,128]{2,1,0:T(8,128)}, u32[]{:S(2)}, u32[]{:S(2)}) async-start(f32[32,152,128]{2,1,0:T(8,128)} %choose.2), calls=%async_computation.2 | async-start | bytes 4980736 | tf_op jit(solution)/shard_map/all_to_all | solution.py:501
  40.5 4.2 %copy-start = (f32[296,64]{1,0:T(8,128)S(1)}, f32[296,64]{1,0:T(8,128)}, u32[]{:S(2)}) copy-start(f32[296,64]{1,0:T(8,128)} %coarse.1) | copy-start | bytes 227332
  40.5 4.2 %collective-permute-start = (f32[296,64]{1,0:T(8,128)}, f32[296,64]{1,0:T(8,128)S(1)}, u32[]{:S(2)}, u32[]{:S(2)}) collective-permute-start(f32[296,64]{1,0:T(8,128)} %coarse.1), channel_id=1, source_target_pairs={{0,1},{1,0},{2,3},{3,2},{4,5},{5,4},{6,7},{7,6},{8,9},{9,8},{10,11... | collective-permute-start | bytes 227336 | tf_op jit(solution)/shard_map/ppermute | solution.py:520
  45.4 31.3 %collective-permute-start.1 = (f32[296,64]{1,0:T(8,128)}, f32[296,64]{1,0:T(8,128)}, u32[]{:S(2)}, u32[]{:S(2)}) collective-permute-start(f32[296,64]{1,0:T(8,128)} %add.73), channel_id=1, source_target_pairs={{0,2},{1,3},{2,0},{3,1},{4,6},{5,7},{6,4},{7,5},{8,10},{9,11},{10,... | collective-permute-start | bytes 227336 | tf_op jit(solution)/shard_map/ppermute | solution.py:520
  77.8 16.4 %copy-start.3 = (pred[32,16]{1,0:T(8,128)(4,1)S(1)}, pred[32,16]{1,0:T(8,128)(4,1)}, u32[]{:S(2)}) copy-start(pred[32,16]{1,0:T(8,128)(4,1)} %copy-done.2) | copy-start | bytes 1540
  90.0 61.4 %all-to-all-start.1 = ((f32[32,152,128]{2,1,0:T(8,128)}), f32[32,152,128]{2,1,0:T(8,128)}, u32[]{:S(2)}, u32[]{:S(2)}) async-start(f32[32,152,128]{2,1,0:T(8,128)} %choose.3), calls=%async_computation.1 | async-start | bytes 4980736 | tf_op jit(solution)/shard_map/all_to_all | solution.py:501
  94.3 0.5 copy-start.5
